TPU v7x, 32 devices: a whole 2x2x4 slice. The times are simulated.
32 devices in a mesh: view: 8 (over z, core), head: 4 (over y, x).
Axes of the slice: x: 2, y: 2, z: 4, core: 2. Of those that a mesh axis runs over, the one named last changes fastest.
Arguments:
- tokens: bfloat16 [16, 512, 1024], P('view', 'head'), may hold values from -6 to 6
- w_qkv_frame: bfloat16 [1024, 3072], replicated, may hold values from -2 to 2
- w_out_frame: bfloat16 [1024, 1024], replicated, may hold values from -0.1875 to 0.1875
- w_qkv_global: bfloat16 [1024, 3072], replicated, may hold values from -2 to 2
- w_out_global: bfloat16 [1024, 1024], replicated, may hold values from -0.1875 to 0.1875
Outputs:
- result: bfloat16 [16, 512, 1024], P('view', 'head')
All inputs are finite; a program needn't handle non-finite values.
Results may differ from a plain program's by a relative error of at most 0.012.
Values may be sent and summed in bfloat16 or wider, within the bound.
A program may use at most 128 MiB of HBM per device.

v0:
```python
import jax
import jax.numpy as jnp
from jax import lax
from jax.sharding import PartitionSpec as P

HEAD = 64


def normalize(stream):
    widened = stream.astype(jnp.float32)
    center = jnp.mean(widened, axis=-1, keepdims=True)
    spread = jnp.mean(jnp.square(widened - center), axis=-1, keepdims=True)
    return ((widened - center) * lax.rsqrt(spread + 1e-06)).astype(jnp.bfloat16)


def on_device(tokens, w_qkv_frame, w_out_frame, w_qkv_global, w_out_global):
    view_here, rows_here, model_dim = tokens.shape
    head_cols = model_dim // lax.axis_size("head")
    heads_here = head_cols // HEAD
    scale_factor = HEAD ** (-0.5)

    def qkv_rows(stream, weight):
        normed = normalize(stream).reshape(view_here * rows_here, model_dim)
        packed = jnp.dot(normed, weight, preferred_element_type=jnp.float32).astype(jnp.bfloat16)
        return packed.reshape(view_here, rows_here, 3, model_dim)

    def project_out(attended, weight, residual):
        rows_back = lax.all_to_all(attended, "head", split_axis=1, concat_axis=2, tiled=True)
        added_out = jnp.dot(
            rows_back.reshape(view_here * rows_here, model_dim),
            weight,
            preferred_element_type=jnp.float32,
        ).reshape(view_here, rows_here, model_dim)
        return (residual.astype(jnp.float32) + added_out).astype(jnp.bfloat16)

    packed_frame = qkv_rows(tokens, w_qkv_frame)
    packed = lax.all_to_all(packed_frame, "head", split_axis=3, concat_axis=1, tiled=True)
    count_views = packed.shape[0]
    seq_len = packed.shape[1]
    split_heads = packed.reshape(count_views, seq_len, 3, heads_here, HEAD)
    scores = (
        jnp.einsum(
            "vqhd,vkhd->vhqk",
            split_heads[:, :, 0],
            split_heads[:, :, 1],
            preferred_element_type=jnp.float32,
        )
        * scale_factor
    )
    top_score = jnp.max(scores, axis=-1, keepdims=True)
    exp_terms = jnp.exp(scores - top_score)
    row_sum = jnp.sum(exp_terms, axis=-1)
    shares = exp_terms.astype(jnp.bfloat16)
    mixed_out = jnp.einsum(
        "vhqk,vkhd->vqhd", shares, split_heads[:, :, 2], preferred_element_type=jnp.float32
    )
    mixed_out = mixed_out / jnp.transpose(row_sum, (0, 2, 1))[..., None]
    frame_mixed = mixed_out.astype(jnp.bfloat16).reshape(count_views, seq_len, head_cols)
    after_frame = project_out(frame_mixed, w_out_frame, tokens)
    packed_global = lax.all_to_all(
        qkv_rows(after_frame, w_qkv_global), "head", split_axis=3, concat_axis=1, tiled=True
    )
    view_cnt, seq_len = (packed_global.shape[0], packed_global.shape[1])
    query_rows = view_cnt * seq_len
    queries = packed_global[:, :, 0].reshape(query_rows, heads_here, HEAD)
    key_rows = packed_global[:, :, 1].reshape(query_rows, head_cols)
    value_rows = packed_global[:, :, 2].reshape(query_rows, head_cols)
    start_state = (
        jnp.full((heads_here, query_rows), -1e30, jnp.float32),
        jnp.zeros((heads_here, query_rows), jnp.float32),
        jnp.zeros((query_rows, heads_here, HEAD), jnp.float32),
    )
    key_piece = lax.all_gather(key_rows, "view", axis=0, tiled=True)
    value_piece = lax.all_gather(value_rows, "view", axis=0, tiled=True)
    piece_len = key_piece.shape[0]

    def step_block(block_idx, running):
        peak_old, sum_old, accum_old = running
        key_blk = lax.dynamic_slice_in_dim(key_piece, block_idx * query_rows, query_rows, 0)
        value_blk = lax.dynamic_slice_in_dim(value_piece, block_idx * query_rows, query_rows, 0)
        key_blk = key_blk.reshape(query_rows, heads_here, HEAD)
        value_blk = value_blk.reshape(query_rows, heads_here, HEAD)
        scores = (
            jnp.einsum("qhd,khd->hqk", queries, key_blk, preferred_element_type=jnp.float32)
            * scale_factor
        )
        peak_new = jnp.maximum(peak_old, jnp.max(scores, axis=-1))
        decay_old = jnp.exp(peak_old - peak_new)
        exp_terms = jnp.exp(scores - peak_new[..., None])
        sum_new = sum_old * decay_old + jnp.sum(exp_terms, axis=-1)
        mixed_out = jnp.einsum(
            "hqk,khd->qhd",
            exp_terms.astype(jnp.bfloat16),
            value_blk,
            preferred_element_type=jnp.float32,
        )
        accum_new = accum_old * jnp.transpose(decay_old)[..., None] + mixed_out
        return (peak_new, sum_new, accum_new)

    peak_fin, sum_fin, accum_fin = lax.fori_loop(
        0, piece_len // query_rows, step_block, start_state
    )
    global_mixed = (accum_fin / jnp.transpose(sum_fin)[..., None]).astype(jnp.bfloat16)
    global_mixed = global_mixed.reshape(view_cnt, seq_len, head_cols)
    return project_out(global_mixed, w_out_global, after_frame)


def solution(mesh):
    return jax.shard_map(
        on_device,
        mesh=mesh,
        in_specs=(P("view", "head", None), P(), P(), P(), P()),
        out_specs=P("view", "head", None),
        check_vma=False,
    )
```

profile of v0, /device:TPU:16, one launch (start us, length us, event | category | flops | bytes accessed | tf_op | source)
XLA Modules:
  0.0 465.4 jit_solution(10510375491386314761)
XLA Ops:
  6.5 1.3 convert_reduce_fusion.1
  7.9 1.3 fusion.43
  9.2 1.3 fusion.44
  10.5 5.8 %convolution_convert_fusion.1 = bf16[256,3072]{1,0:T(8,128)(2,1)} fusion(bf16[256,1024]{1,0:T(8,128)(2,1)S(1)} %bitcast.125, bf16[1024,3072]{1,0:T(8,128)(2,1)} %param.8), kind=kOutput, calls=%fused_computation.25 | convolution fusion | flops 1611399168 | bytes 8388608 | tf_op jit(solution)/shard_map/dot_general | solution.py:24
  16.2 5.6 %reshape.86 = bf16[2,128,3,1024]{3,2,1,0:T(4,128)(2,1)} reshape(bf16[256,3072]{1,0:T(8,128)(2,1)} %convolution_convert_fusion.1) | data formatting | bytes 3145728 | tf_op jit(solution)/shard_map/reshape | solution.py:25
  21.8 6.2 %copy.69 = bf16[2,128,3,1024]{1,0,2,3:T(2,128)(2,1)} copy(bf16[2,128,3,1024]{3,2,1,0:T(4,128)(2,1)} %reshape.86) | data formatting | bytes 3145728 | tf_op jit(solution)/shard_map/reshape | solution.py:25
  28.0 23.6 %all_to_all.63 = bf16[2,128,3,1024]{1,0,2,3:T(2,128)(2,1)S(1)} all-to-all(bf16[2,128,3,1024]{1,0,2,3:T(2,128)(2,1)} %copy.69), channel_id=1, replica_groups=mesh['view'=8,'head'=4] {'head'}, dimensions={3} | all-to-all | bytes 3145728 | tf_op jit(solution)/shard_map/all_to_all | solution.py:37
  51.8 2.4 copy.71
  54.2 3.6 reshape.77
  57.8 2.5 multiply_reduce_fusion
  60.4 1.4 fusion.14
  61.8 3.5 divide_convert_fusion.1
  65.3 1.3 copy.73
  66.6 9.6 %all_to_all.64 = bf16[2,512,256]{2,0,1:T(2,128)(2,1)S(1)} all-to-all(bf16[2,512,256]{2,0,1:T(2,128)(2,1)S(1)} %copy.73), channel_id=1, replica_groups=mesh['view'=8,'head'=4] {'head'}, dimensions={1} | all-to-all | bytes 1048576 | tf_op jit(solution)/shard_map/all_to_all | solution.py:28
  76.7 1.2 dot_general.37
  77.8 1.8 convert_reduce_fusion
  80.2 5.7 %convolution_convert_fusion = bf16[256,3072]{1,0:T(8,128)(2,1)} fusion(bf16[256,1024]{1,0:T(8,128)(2,1)S(1)} %bitcast.126, bf16[1024,3072]{1,0:T(8,128)(2,1)} %param.10), kind=kOutput, calls=%fused_computation.24 | convolution fusion | flops 1611399168 | bytes 8388608 | tf_op jit(solution)/shard_map/dot_general | solution.py:24
  86.0 4.6 reshape.87
  90.6 4.1 copy.76
  94.7 20.7 %all_to_all.65 = bf16[2,128,3,1024]{1,0,2,3:T(2,128)(2,1)S(1)} all-to-all(bf16[2,128,3,1024]{1,0,2,3:T(2,128)(2,1)} %copy.76), channel_id=1, replica_groups=mesh['view'=8,'head'=4] {'head'}, dimensions={3} | all-to-all | bytes 3145728 | tf_op jit(solution)/shard_map/all_to_all | solution.py:60
  115.4 1.4 copy.77
  116.8 1.7 copy.78
  119.4 2.0 copy.79
  121.5 1.0 copy.81
  123.4 43.4 %all-gather.3.cloned.1.call-done = bf16[8192,256]{0,1:T(8,128)(2,1)} async-done(((bf16[1024,256]{0,1:T(8,128)(2,1)}), bf16[8192,256]{0,1:T(8,128)(2,1)}) %all-gather.3.cloned.1.call-update) | async-done | bytes 4194320 | tf_op jit(solution)/shard_map/all_gather | solution.py:73
  166.8 47.3 %all-gather.5.cloned.1.call-done = bf16[8192,256]{0,1:T(8,128)(2,1)} async-done(((bf16[1024,256]{0,1:T(8,128)(2,1)}), bf16[8192,256]{0,1:T(8,128)(2,1)}) %all-gather.5.cloned.1.call-update) | async-done | bytes 4194320 | tf_op jit(solution)/shard_map/all_gather | solution.py:74
  214.1 223.8 %while.18 = (s32[]{:T(128)}, f32[4,1024]{1,0:T(4,128)S(1)}, f32[4,1024]{1,0:T(4,128)S(1)}, f32[1024,4,64]{0,2,1:T(8,128)}, bf16[8192,256]{0,1:T(8,128)(2,1)}, /*...) while((s32[]{:T(128)}, f32[4,1024]{1,0:T(4,128)S(1)}, ...), condition=%wide.region_9.0_spmd.clone, body=%wide.region_6.0_spmd.clone.sunk | while | flops 1108107264 | bytes 56361128 | solution.py:100
  214.1 1.3 constant_dynamic-slice_fusion.3
  215.4 8.1 %bitcast_reduce_fusion.2 = (f32[4,1024]{1,0:T(4,128)S(1)}, f32[4,1024,1024]{2,1,0:T(8,128)}) fusion(bf16[1024,4,64]{0,2,1:T(8,128)(2,1)S(1)} %bitcast.113, bf16[1024,4,64]{0,2,1:T(8,128)(2,1)S(1)} %get-tuple-element.272), kind=kOutput, calls=%fused_computation.1.clone.1 | convolution fusion | flops 545255424 | bytes 17842176 | tf_op jit(solution)/shard_map/while/body/eval_jaxpr/qhd,khd->hqk/dot_general | solution.py:84
  223.5 9.8 %fusion.74 = f32[1024,4,64]{0,2,1:T(8,128)} fusion(bf16[1024,4,64]{0,2,1:T(8,128)(2,1)S(1)} %bitcast.114, f32[4,1024,1024]{2,1,0:T(8,128)} %get-tuple-element.242, f32[4,1024]{1,0:T(4,128)S(1)} %get-tuple-element.268, f32[1024,4,64]{0,2,1:T(8,128)} %get-tuple-element.259, f32[1024,4]{0,1:T(4,128)S(1)} %get-tuple-element.244, pred[]{:T(512)S(6)} %compare.3), kind=kOutput, calls=%fused_computation.7.clone.1 | convolution fusion | flops 550240256 | bytes 19431424 | tf_op jit(solution)/shard_map/while/body/eval_jaxpr/hqk,khd->qhd/dot_general | solution.py:91
  233.3 8.5 %fusion.72 = f32[4,1024]{1,0:T(4,128)S(1)} fusion(f32[4,1024,1024]{2,1,0:T(8,128)} %get-tuple-element.242, f32[4,1024]{1,0:T(4,128)S(1)} %get-tuple-element.268), kind=kLoop, calls=%fused_computation.4.clone.1 | loop fusion | flops 12578816 | bytes 16809984 | tf_op jit(solution)/shard_map/while/body/eval_jaxpr/reduce_sum | solution.py:90
  241.9 1.3 constant_dynamic-slice_fusion.3
  243.2 8.1 %bitcast_reduce_fusion.2 = (f32[4,1024]{1,0:T(4,128)S(1)}, f32[4,1024,1024]{2,1,0:T(8,128)}) fusion(bf16[1024,4,64]{0,2,1:T(8,128)(2,1)S(1)} %bitcast.113, bf16[1024,4,64]{0,2,1:T(8,128)(2,1)S(1)} %get-tuple-element.272), kind=kOutput, calls=%fused_computation.1.clone.1 | convolution fusion | flops 545255424 | bytes 17842176 | tf_op jit(solution)/shard_map/while/body/eval_jaxpr/qhd,khd->hqk/dot_general | solution.py:84
  251.3 10.0 %fusion.74 = f32[1024,4,64]{0,2,1:T(8,128)} fusion(bf16[1024,4,64]{0,2,1:T(8,128)(2,1)S(1)} %bitcast.114, f32[4,1024,1024]{2,1,0:T(8,128)} %get-tuple-element.242, f32[4,1024]{1,0:T(4,128)S(1)} %get-tuple-element.268, f32[1024,4,64]{0,2,1:T(8,128)} %get-tuple-element.259, f32[1024,4]{0,1:T(4,128)S(1)} %get-tuple-element.244, pred[]{:T(512)S(6)} %compare.3), kind=kOutput, calls=%fused_computation.7.clone.1 | convolution fusion | flops 550240256 | bytes 19431424 | tf_op jit(solution)/shard_map/while/body/eval_jaxpr/hqk,khd->qhd/dot_general | solution.py:91
  261.3 8.5 %fusion.72 = f32[4,1024]{1,0:T(4,128)S(1)} fusion(f32[4,1024,1024]{2,1,0:T(8,128)} %get-tuple-element.242, f32[4,1024]{1,0:T(4,128)S(1)} %get-tuple-element.268), kind=kLoop, calls=%fused_computation.4.clone.1 | loop fusion | flops 12578816 | bytes 16809984 | tf_op jit(solution)/shard_map/while/body/eval_jaxpr/reduce_sum | solution.py:90
  269.9 1.3 constant_dynamic-slice_fusion.3
  271.2 8.1 %bitcast_reduce_fusion.2 = (f32[4,1024]{1,0:T(4,128)S(1)}, f32[4,1024,1024]{2,1,0:T(8,128)}) fusion(bf16[1024,4,64]{0,2,1:T(8,128)(2,1)S(1)} %bitcast.113, bf16[1024,4,64]{0,2,1:T(8,128)(2,1)S(1)} %get-tuple-element.272), kind=kOutput, calls=%fused_computation.1.clone.1 | convolution fusion | flops 545255424 | bytes 17842176 | tf_op jit(solution)/shard_map/while/body/eval_jaxpr/qhd,khd->hqk/dot_general | solution.py:84
  279.3 10.0 %fusion.74 = f32[1024,4,64]{0,2,1:T(8,128)} fusion(bf16[1024,4,64]{0,2,1:T(8,128)(2,1)S(1)} %bitcast.114, f32[4,1024,1024]{2,1,0:T(8,128)} %get-tuple-element.242, f32[4,1024]{1,0:T(4,128)S(1)} %get-tuple-element.268, f32[1024,4,64]{0,2,1:T(8,128)} %get-tuple-element.259, f32[1024,4]{0,1:T(4,128)S(1)} %get-tuple-element.244, pred[]{:T(512)S(6)} %compare.3), kind=kOutput, calls=%fused_computation.7.clone.1 | convolution fusion | flops 550240256 | bytes 19431424 | tf_op jit(solution)/shard_map/while/body/eval_jaxpr/hqk,khd->qhd/dot_general | solution.py:91
  289.3 8.5 %fusion.72 = f32[4,1024]{1,0:T(4,128)S(1)} fusion(f32[4,1024,1024]{2,1,0:T(8,128)} %get-tuple-element.242, f32[4,1024]{1,0:T(4,128)S(1)} %get-tuple-element.268), kind=kLoop, calls=%fused_computation.4.clone.1 | loop fusion | flops 12578816 | bytes 16809984 | tf_op jit(solution)/shard_map/while/body/eval_jaxpr/reduce_sum | solution.py:90
  297.9 1.3 constant_dynamic-slice_fusion.3
  299.2 8.1 %bitcast_reduce_fusion.2 = (f32[4,1024]{1,0:T(4,128)S(1)}, f32[4,1024,1024]{2,1,0:T(8,128)}) fusion(bf16[1024,4,64]{0,2,1:T(8,128)(2,1)S(1)} %bitcast.113, bf16[1024,4,64]{0,2,1:T(8,128)(2,1)S(1)} %get-tuple-element.272), kind=kOutput, calls=%fused_computation.1.clone.1 | convolution fusion | flops 545255424 | bytes 17842176 | tf_op jit(solution)/shard_map/while/body/eval_jaxpr/qhd,khd->hqk/dot_general | solution.py:84
  307.3 10.0 %fusion.74 = f32[1024,4,64]{0,2,1:T(8,128)} fusion(bf16[1024,4,64]{0,2,1:T(8,128)(2,1)S(1)} %bitcast.114, f32[4,1024,1024]{2,1,0:T(8,128)} %get-tuple-element.242, f32[4,1024]{1,0:T(4,128)S(1)} %get-tuple-element.268, f32[1024,4,64]{0,2,1:T(8,128)} %get-tuple-element.259, f32[1024,4]{0,1:T(4,128)S(1)} %get-tuple-element.244, pred[]{:T(512)S(6)} %compare.3), kind=kOutput, calls=%fused_computation.7.clone.1 | convolution fusion | flops 550240256 | bytes 19431424 | tf_op jit(solution)/shard_map/while/body/eval_jaxpr/hqk,khd->qhd/dot_general | solution.py:91
  317.3 8.5 %fusion.72 = f32[4,1024]{1,0:T(4,128)S(1)} fusion(f32[4,1024,1024]{2,1,0:T(8,128)} %get-tuple-element.242, f32[4,1024]{1,0:T(4,128)S(1)} %get-tuple-element.268), kind=kLoop, calls=%fused_computation.4.clone.1 | loop fusion | flops 12578816 | bytes 16809984 | tf_op jit(solution)/shard_map/while/body/eval_jaxpr/reduce_sum | solution.py:90
  325.9 1.3 constant_dynamic-slice_fusion.3
  327.2 8.1 %bitcast_reduce_fusion.2 = (f32[4,1024]{1,0:T(4,128)S(1)}, f32[4,1024,1024]{2,1,0:T(8,128)}) fusion(bf16[1024,4,64]{0,2,1:T(8,128)(2,1)S(1)} %bitcast.113, bf16[1024,4,64]{0,2,1:T(8,128)(2,1)S(1)} %get-tuple-element.272), kind=kOutput, calls=%fused_computation.1.clone.1 | convolution fusion | flops 545255424 | bytes 17842176 | tf_op jit(solution)/shard_map/while/body/eval_jaxpr/qhd,khd->hqk/dot_general | solution.py:84
  335.3 10.0 %fusion.74 = f32[1024,4,64]{0,2,1:T(8,128)} fusion(bf16[1024,4,64]{0,2,1:T(8,128)(2,1)S(1)} %bitcast.114, f32[4,1024,1024]{2,1,0:T(8,128)} %get-tuple-element.242, f32[4,1024]{1,0:T(4,128)S(1)} %get-tuple-element.268, f32[1024,4,64]{0,2,1:T(8,128)} %get-tuple-element.259, f32[1024,4]{0,1:T(4,128)S(1)} %get-tuple-element.244, pred[]{:T(512)S(6)} %compare.3), kind=kOutput, calls=%fused_computation.7.clone.1 | convolution fusion | flops 550240256 | bytes 19431424 | tf_op jit(solution)/shard_map/while/body/eval_jaxpr/hqk,khd->qhd/dot_general | solution.py:91
  345.3 8.5 %fusion.72 = f32[4,1024]{1,0:T(4,128)S(1)} fusion(f32[4,1024,1024]{2,1,0:T(8,128)} %get-tuple-element.242, f32[4,1024]{1,0:T(4,128)S(1)} %get-tuple-element.268), kind=kLoop, calls=%fused_computation.4.clone.1 | loop fusion | flops 12578816 | bytes 16809984 | tf_op jit(solution)/shard_map/while/body/eval_jaxpr/reduce_sum | solution.py:90
  353.9 1.3 constant_dynamic-slice_fusion.3
  355.2 8.1 %bitcast_reduce_fusion.2 = (f32[4,1024]{1,0:T(4,128)S(1)}, f32[4,1024,1024]{2,1,0:T(8,128)}) fusion(bf16[1024,4,64]{0,2,1:T(8,128)(2,1)S(1)} %bitcast.113, bf16[1024,4,64]{0,2,1:T(8,128)(2,1)S(1)} %get-tuple-element.272), kind=kOutput, calls=%fused_computation.1.clone.1 | convolution fusion | flops 545255424 | bytes 17842176 | tf_op jit(solution)/shard_map/while/body/eval_jaxpr/qhd,khd->hqk/dot_general | solution.py:84
  363.3 10.0 %fusion.74 = f32[1024,4,64]{0,2,1:T(8,128)} fusion(bf16[1024,4,64]{0,2,1:T(8,128)(2,1)S(1)} %bitcast.114, f32[4,1024,1024]{2,1,0:T(8,128)} %get-tuple-element.242, f32[4,1024]{1,0:T(4,128)S(1)} %get-tuple-element.268, f32[1024,4,64]{0,2,1:T(8,128)} %get-tuple-element.259, f32[1024,4]{0,1:T(4,128)S(1)} %get-tuple-element.244, pred[]{:T(512)S(6)} %compare.3), kind=kOutput, calls=%fused_computation.7.clone.1 | convolution fusion | flops 550240256 | bytes 19431424 | tf_op jit(solution)/shard_map/while/body/eval_jaxpr/hqk,khd->qhd/dot_general | solution.py:91
  373.3 8.5 %fusion.72 = f32[4,1024]{1,0:T(4,128)S(1)} fusion(f32[4,1024,1024]{2,1,0:T(8,128)} %get-tuple-element.242, f32[4,1024]{1,0:T(4,128)S(1)} %get-tuple-element.268), kind=kLoop, calls=%fused_computation.4.clone.1 | loop fusion | flops 12578816 | bytes 16809984 | tf_op jit(solution)/shard_map/while/body/eval_jaxpr/reduce_sum | solution.py:90
  381.9 1.3 constant_dynamic-slice_fusion.3
  383.2 8.1 %bitcast_reduce_fusion.2 = (f32[4,1024]{1,0:T(4,128)S(1)}, f32[4,1024,1024]{2,1,0:T(8,128)}) fusion(bf16[1024,4,64]{0,2,1:T(8,128)(2,1)S(1)} %bitcast.113, bf16[1024,4,64]{0,2,1:T(8,128)(2,1)S(1)} %get-tuple-element.272), kind=kOutput, calls=%fused_computation.1.clone.1 | convolution fusion | flops 545255424 | bytes 17842176 | tf_op jit(solution)/shard_map/while/body/eval_jaxpr/qhd,khd->hqk/dot_general | solution.py:84
  391.3 10.0 %fusion.74 = f32[1024,4,64]{0,2,1:T(8,128)} fusion(bf16[1024,4,64]{0,2,1:T(8,128)(2,1)S(1)} %bitcast.114, f32[4,1024,1024]{2,1,0:T(8,128)} %get-tuple-element.242, f32[4,1024]{1,0:T(4,128)S(1)} %get-tuple-element.268, f32[1024,4,64]{0,2,1:T(8,128)} %get-tuple-element.259, f32[1024,4]{0,1:T(4,128)S(1)} %get-tuple-element.244, pred[]{:T(512)S(6)} %compare.3), kind=kOutput, calls=%fused_computation.7.clone.1 | convolution fusion | flops 550240256 | bytes 19431424 | tf_op jit(solution)/shard_map/while/body/eval_jaxpr/hqk,khd->qhd/dot_general | solution.py:91
  401.4 8.5 %fusion.72 = f32[4,1024]{1,0:T(4,128)S(1)} fusion(f32[4,1024,1024]{2,1,0:T(8,128)} %get-tuple-element.242, f32[4,1024]{1,0:T(4,128)S(1)} %get-tuple-element.268), kind=kLoop, calls=%fused_computation.4.clone.1 | loop fusion | flops 12578816 | bytes 16809984 | tf_op jit(solution)/shard_map/while/body/eval_jaxpr/reduce_sum | solution.py:90
  409.9 1.3 constant_dynamic-slice_fusion.3
  411.2 8.1 %bitcast_reduce_fusion.2 = (f32[4,1024]{1,0:T(4,128)S(1)}, f32[4,1024,1024]{2,1,0:T(8,128)}) fusion(bf16[1024,4,64]{0,2,1:T(8,128)(2,1)S(1)} %bitcast.113, bf16[1024,4,64]{0,2,1:T(8,128)(2,1)S(1)} %get-tuple-element.272), kind=kOutput, calls=%fused_computation.1.clone.1 | convolution fusion | flops 545255424 | bytes 17842176 | tf_op jit(solution)/shard_map/while/body/eval_jaxpr/qhd,khd->hqk/dot_general | solution.py:84
  419.3 10.0 %fusion.74 = f32[1024,4,64]{0,2,1:T(8,128)} fusion(bf16[1024,4,64]{0,2,1:T(8,128)(2,1)S(1)} %bitcast.114, f32[4,1024,1024]{2,1,0:T(8,128)} %get-tuple-element.242, f32[4,1024]{1,0:T(4,128)S(1)} %get-tuple-element.268, f32[1024,4,64]{0,2,1:T(8,128)} %get-tuple-element.259, f32[1024,4]{0,1:T(4,128)S(1)} %get-tuple-element.244, pred[]{:T(512)S(6)} %compare.3), kind=kOutput, calls=%fused_computation.7.clone.1 | convolution fusion | flops 550240256 | bytes 19431424 | tf_op jit(solution)/shard_map/while/body/eval_jaxpr/hqk,khd->qhd/dot_general | solution.py:91
  429.4 8.5 %fusion.72 = f32[4,1024]{1,0:T(4,128)S(1)} fusion(f32[4,1024,1024]{2,1,0:T(8,128)} %get-tuple-element.242, f32[4,1024]{1,0:T(4,128)S(1)} %get-tuple-element.268), kind=kLoop, calls=%fused_computation.4.clone.1 | loop fusion | flops 12578816 | bytes 16809984 | tf_op jit(solution)/shard_map/while/body/eval_jaxpr/reduce_sum | solution.py:90
  437.9 1.5 divide_convert_fusion
  439.4 1.2 reshape.81
  440.6 2.4 copy.82
  442.9 12.4 %all_to_all.66 = bf16[2,512,256]{2,0,1:T(2,128)(2,1)S(1)} all-to-all(bf16[2,512,256]{2,0,1:T(2,128)(2,1)S(1)} %copy.82), channel_id=1, replica_groups=mesh['view'=8,'head'=4] {'head'}, dimensions={1} | all-to-all | bytes 1048576 | tf_op jit(solution)/shard_map/all_to_all | solution.py:28
  455.5 3.1 fusion.34
  (50 shorter events, 3.6 us)
Async XLA Ops:
  6.5 71.3 %copy-start = (bf16[1024,1024]{1,0:T(8,128)(2,1)S(1)}, bf16[1024,1024]{1,0:T(8,128)(2,1)}, u32[]{:S(2)}) copy-start(bf16[1024,1024]{1,0:T(8,128)(2,1)} %param.9) | copy-start | bytes 6291460
  6.5 160.3 %all-gather.3.cloned.1.call-start = ((), (), s32[]{:S(2)}) async-start(), calls=%async_computation.4 | async-start | bytes 4718592 | tf_op jit(solution)/shard_map/all_gather | solution.py:73
  61.7 16.1 %copy-start.2 = (bf16[2,128,1024]{2,1,0:T(8,128)(2,1)S(1)}, bf16[2,128,1024]{2,1,0:T(8,128)(2,1)}, u32[]{:S(2)}) copy-start(bf16[2,128,1024]{2,1,0:T(8,128)(2,1)} %param.7) | copy-start | bytes 1572868
  121.4 92.7 %all-gather.5.cloned.1.call-start = ((), (), s32[]{:S(2)}) async-start(), calls=%async_computation.5 | async-start | bytes 4718592 | tf_op jit(solution)/shard_map/all_gather | solution.py:74
  437.9 20.6 %copy-start.1 = (bf16[1024,1024]{1,0:T(8,128)(2,1)S(1)}, bf16[1024,1024]{1,0:T(8,128)(2,1)}, u32[]{:S(2)}) copy-start(bf16[1024,1024]{1,0:T(8,128)(2,1)} %param.9) | copy-start | bytes 6291460
Sparse Core Ops, SparseCore 0:
  121.6 45.2 all-gather.2
  168.4 45.6 all-gather.4
where the time goes:
time: 470 us; the launch traced here: 465 us
  matrix products  167 us (36%)
  waiting for transfers between devices  90.7 us (19%)
  other arithmetic  75.8 us (16%)
  blocking collectives  66.3 us (14%)
  local copies, waits for them, and re-layouts  51.4 us (11%)
  between operations  13.6 us (3%)
    dot_general x8, matrix products, step_block(): jnp.einsum('hqk,khd->qhd', exp_terms.astype(jnp.bfloat16), value_blk, pre...  80 us
    reduce_sum x8, other arithmetic, step_block(): sum_new = sum_old * decay_old + jnp.sum(exp_terms, axis=-1)  68 us
    dot_general x8, matrix products, step_block(): jnp.einsum('qhd,khd->hqk', queries, key_blk, preferred_element_type=jnp.f...  64.8 us
    all_gather x1, waiting for transfers between devices, on_device(): value_piece = lax.all_gather(value_rows, 'view', axis=0, tiled=True)  47.3 us
    all_gather x1, waiting for transfers between devices, on_device(): key_piece = lax.all_gather(key_rows, 'view', axis=0, tiled=True)  43.4 us
    all_to_all x1, blocking collectives, on_device(): lax.all_to_all(packed_frame, 'head', split_axis=3, concat_axis=1, tiled=T...  23.6 us
    all_to_all x2, blocking collectives, project_out(): lax.all_to_all(attended, 'head', split_axis=1, concat_axis=2, tiled=True)  22 us
    all_to_all x1, blocking collectives, on_device(): lax.all_to_all(qkv_rows(after_frame, w_qkv_global), 'head', split_axis=3,...  20.7 us
  transfers between devices with their start and end apart: 2, of which 2 were waited for; matrix products, arithmetic and copies ran while one was open for 0% of the time, Pallas kernels for 0%

commit v1 on v0

v1 whole, which is shorter than its diff:
```python
import functools
import math

import jax
import jax.numpy as jnp
from jax import lax
from jax.experimental import pallas as pl
from jax.experimental.pallas import tpu as pltpu
from jax.sharding import PartitionSpec as P

HEAD = 64
LANES = 128
SCORE_SCALE = HEAD ** (-0.5) * math.log2(math.e)
VMEM_BYTES = 56 * 2**20


def normalize(stream):
    widened = stream.astype(jnp.float32)
    center = jnp.mean(widened, axis=-1, keepdims=True)
    spread = jnp.mean(jnp.square(widened - center), axis=-1, keepdims=True)
    return ((widened - center) * lax.rsqrt(spread + 1e-06)).astype(jnp.bfloat16)


def frame_kernel(q_ref, k_ref, v_ref, o_ref):
    outs = []
    for head in range(q_ref.shape[1] // HEAD):
        cols = slice(head * HEAD, (head + 1) * HEAD)
        scores = lax.dot_general(
            q_ref[:, cols], k_ref[:, cols], (((1,), (1,)), ((), ())),
            preferred_element_type=jnp.float32,
        )
        terms = jnp.exp2(scores - jnp.max(scores, axis=1, keepdims=True))
        total = jnp.sum(terms, axis=1, keepdims=True)
        mixed = jnp.dot(
            terms.astype(jnp.bfloat16), v_ref[:, cols], preferred_element_type=jnp.float32
        )
        outs.append(mixed / total)
    o_ref[...] = jnp.concatenate(outs, axis=1).astype(jnp.bfloat16)


def frame_attention(queries, keys, values):
    rows, cols = queries.shape
    spec = pl.BlockSpec((rows, LANES), lambda i: (0, i))
    return pl.pallas_call(
        frame_kernel,
        grid=(cols // LANES,),
        in_specs=[spec] * 3,
        out_specs=spec,
        out_shape=jax.ShapeDtypeStruct((rows, cols), jnp.bfloat16),
        compiler_params=pltpu.CompilerParams(vmem_limit_bytes=VMEM_BYTES),
        name="frame_attention",
    )(queries, keys, values)


def global_kernel(key_step, q_ref, kv_ref, o_ref, keys, values):
    pieces, _, head, width = kv_ref.shape

    @pl.when(pl.program_id(0) == 0)
    def _():
        def lay_out(piece, carry):
            at = pl.ds(pl.multiple_of(piece * width, width), width)
            keys[:, at] = kv_ref[piece, 0]
            wide = jnp.concatenate(
                [kv_ref[piece, 1], jnp.ones((LANES - head, width), jnp.bfloat16)], axis=0
            )
            values[at, :] = wide.T
            return carry

        lax.fori_loop(0, pieces, lay_out, 0)

    blocks = q_ref.shape[0]
    queries = jnp.concatenate([q_ref[i, 0] for i in range(blocks)], axis=1).T
    rows = queries.shape[0]
    peak = jnp.full((rows, 1), -1e30, jnp.float32)
    accum = jnp.zeros((rows, LANES), jnp.float32)
    for start in range(0, pieces * width, key_step):
        scores = jnp.dot(
            queries, keys[:, start : start + key_step], preferred_element_type=jnp.float32
        )
        peak_new = jnp.maximum(peak, jnp.max(scores, axis=1, keepdims=True))
        terms = jnp.exp2(scores - peak_new).astype(jnp.bfloat16)
        accum = accum * jnp.exp2(peak - peak_new) + jnp.dot(
            terms, values[start : start + key_step, :], preferred_element_type=jnp.float32
        )
        peak = peak_new
    mixed = (accum[:, :head] / accum[:, head : head + 1]).T.astype(jnp.bfloat16)
    for i in range(blocks):
        o_ref[i] = mixed[:, i * width : (i + 1) * width]


def global_attention(packed, key_values, query_step, key_step):
    sources, _, head, width = packed.shape
    pieces = key_values.shape[0]
    blocks = min(sources, max(1, query_step // width))
    key_step = min(key_step, pieces * width)
    return pl.pallas_call(
        functools.partial(global_kernel, key_step),
        grid=(sources // blocks,),
        in_specs=[
            pl.BlockSpec((blocks, 1, head, width), lambda i: (i, 0, 0, 0)),
            pl.BlockSpec((pieces, 2, head, width), lambda i: (0, 0, 0, 0)),
        ],
        out_specs=pl.BlockSpec((blocks, head, width), lambda i: (i, 0, 0)),
        out_shape=jax.ShapeDtypeStruct((sources, head, width), jnp.bfloat16),
        scratch_shapes=[
            pltpu.VMEM((head, pieces * width), jnp.bfloat16),
            pltpu.VMEM((pieces * width, LANES), jnp.bfloat16),
        ],
        compiler_params=pltpu.CompilerParams(vmem_limit_bytes=VMEM_BYTES),
        name="global_attention",
    )(packed, key_values)


def on_device(tokens, w_qkv_frame, w_out_frame, w_qkv_global, w_out_global):
    view_here, rows_here, model_dim = tokens.shape
    head_size, view_size = lax.axis_size("head"), lax.axis_size("view")
    tokens_here = view_here * rows_here

    shares = head_size // view_here
    cols = model_dim // shares
    share = lax.rem(lax.axis_index("head"), shares)
    sent = jnp.repeat(normalize(tokens), shares, axis=0)
    view_rows = lax.all_to_all(sent, "head", split_axis=0, concat_axis=0, tiled=True)
    view_rows = view_rows.reshape(head_size * rows_here, model_dim)

    def project(which):
        weight = lax.dynamic_slice_in_dim(w_qkv_frame, which * model_dim + share * cols, cols, 1)
        return jnp.dot(view_rows, weight, preferred_element_type=jnp.float32)

    frame_mixed = frame_attention(
        (project(0) * SCORE_SCALE).astype(jnp.bfloat16),
        project(1).astype(jnp.bfloat16),
        project(2).astype(jnp.bfloat16),
    )
    back = lax.all_to_all(
        frame_mixed.reshape(head_size, rows_here, cols), "head", split_axis=0, concat_axis=0, tiled=True
    ).reshape(view_here, shares, rows_here, cols)
    added = jnp.dot(
        jnp.transpose(back, (0, 2, 1, 3)).reshape(tokens_here, model_dim),
        w_out_frame,
        preferred_element_type=jnp.float32,
    )
    after_frame = (tokens.astype(jnp.float32).reshape(tokens_here, model_dim) + added).astype(
        jnp.bfloat16
    )

    heads = model_dim // HEAD
    copies = view_size * head_size // heads
    normed = normalize(after_frame)
    packed = lax.dot_general(
        w_qkv_global, normed, (((0,), (1,)), ((), ())), preferred_element_type=jnp.float32
    ).reshape(3, heads, HEAD, tokens_here)
    scale = jnp.array([SCORE_SCALE, 1.0, 1.0], jnp.float32).reshape(3, 1, 1, 1)
    packed = jnp.transpose((packed * scale).astype(jnp.bfloat16), (1, 0, 2, 3))
    groups = [
        [
            (outer * copies + copy) * head_size + inner
            for outer in range(view_size // copies)
            for inner in range(head_size)
        ]
        for copy in range(copies)
    ]
    by_head = lax.all_to_all(
        packed, ("view", "head"), split_axis=0, concat_axis=0, axis_index_groups=groups, tiled=True
    )
    key_values = lax.all_gather(
        by_head[:, 1:],
        "view",
        axis=0,
        axis_index_groups=[
            [outer * copies + copy for copy in range(copies)]
            for outer in range(view_size // copies)
        ],
        tiled=True,
    )
    mixed = global_attention(by_head, key_values, 1024, 1024)
    mixed = lax.all_to_all(
        mixed, ("view", "head"), split_axis=0, concat_axis=0, axis_index_groups=groups, tiled=True
    ).reshape(model_dim, tokens_here)
    added = lax.dot_general(
        mixed, w_out_global, (((0,), (0,)), ((), ())), preferred_element_type=jnp.float32
    )
    result = (after_frame.astype(jnp.float32) + added).astype(jnp.bfloat16)
    return result.reshape(view_here, rows_here, model_dim)


def solution(mesh):
    return jax.shard_map(
        on_device,
        mesh=mesh,
        in_specs=(P("view", "head", None), P(), P(), P(), P()),
        out_specs=P("view", "head", None),
        check_vma=False,
    )
```

time: 470 us -> 199 us (0.42)
  matrix products: 167 us -> 16.9 us
  other arithmetic: 75.8 us -> 6.56 us
  waiting for transfers between devices: 90.7 us -> 24.7 us
  Pallas kernels: 0 us -> 50.8 us
  local copies, waits for them, and re-layouts: 51.4 us -> 7.52 us
  blocking collectives: 66.3 us -> 71.2 us
    dot_general x22 -> x6, matrix products: 167 us -> 16.9 us  [the longest x3 8.21 us: project(): return jnp.dot(view_rows, weight, preferred_element_type=jnp.float32)]
    all_gather x2 -> x1, waiting for transfers between devices: 90.7 us -> 11 us  [on_device(): lax.all_gather(by_head[:, 1:], 'view', axis=0, axis_index_groups=[[outer...]
    reduce_sum x9 -> x0, other arithmetic: 69.4 us -> none  [the longest x8 68 us: step_block(): sum_new = sum_old * decay_old + jnp.sum(exp_terms, axis=-1)]
    pallas_call x0 -> x2, Pallas kernels: none -> 50.8 us  [the longest x1 43.2 us: global_attention(): pl.pallas_call(functools.partial(global_kernel, key_step), grid=(sources...]
    reshape x8 -> x0, local copies, waits for them, and re-layouts: 29 us -> none  [the longest x4 20.5 us: qkv_rows(): return packed.reshape(view_here, rows_here, 3, model_dim)]
    all_to_all x0 -> x1, waiting for transfers between devices: none -> 13.7 us  [on_device(): lax.all_to_all(sent, 'head', split_axis=0, concat_axis=0, tiled=True)]
    dynamic_slice x8 -> x0, local copies, waits for them, and re-layouts: 10.2 us -> none  [step_block(): lax.dynamic_slice_in_dim(value_piece, block_idx * query_rows, query_rows, 0)]
    all_to_all x6 -> x0, local copies, waits for them, and re-layouts: 6.12 us -> none  [the longest x2 3.07 us: on_device(): lax.all_to_all(qkv_rows(after_frame, w_qkv_global), 'head', split_axis=3,...]
where the time goes in v1:
time: 199 us; the launch traced here: 195 us
  blocking collectives  71.2 us (36%)
  Pallas kernels  50.8 us (26%)
  waiting for transfers between devices  24.7 us (12%)
  matrix products  16.9 us (8%)
  between operations  13.5 us (7%)
  local copies, waits for them, and re-layouts  7.52 us (4%)
  other arithmetic  6.56 us (3%)
  starting transfers between devices  3.72 us (2%)
    pallas_call x1, Pallas kernels, global_attention(): pl.pallas_call(functools.partial(global_kernel, key_step), grid=(sources...  43.2 us
    all_to_all x1, blocking collectives, on_device(): lax.all_to_all(packed, ('view', 'head'), split_axis=0, concat_axis=0, axi...  39.3 us
    all_to_all x1, blocking collectives, on_device(): lax.all_to_all(mixed, ('view', 'head'), split_axis=0, concat_axis=0, axis...  20.4 us
    all_to_all x1, waiting for transfers between devices, on_device(): lax.all_to_all(sent, 'head', split_axis=0, concat_axis=0, tiled=True)  13.7 us
    all_to_all x1, blocking collectives, on_device(): lax.all_to_all(frame_mixed.reshape(head_size, rows_here, cols), 'head', s...  11.5 us
    all_gather x1, waiting for transfers between devices, on_device(): lax.all_gather(by_head[:, 1:], 'view', axis=0, axis_index_groups=[[outer...  11 us
    dot_general x3, matrix products, project(): return jnp.dot(view_rows, weight, preferred_element_type=jnp.float32)  8.21 us
    pallas_call x1, Pallas kernels, frame_attention(): pl.pallas_call(frame_kernel, grid=(cols // LANES,), in_specs=[spec] * 3,...  7.56 us
  transfers between devices with their start and end apart: 2, of which 2 were waited for; matrix products, arithmetic and copies ran while one was open for 0% of the time, Pallas kernels for 0%

profile of v1, /device:TPU:16, one launch (start us, length us, event | category | flops | bytes accessed | tf_op | source)
XLA Modules:
  0.0 194.8 jit_solution(6741240698817406529)
XLA Ops:
  6.5 0.0 copy-start
  6.5 1.3 convert_reduce_fusion.1
  7.9 1.3 multiply_reduce_fusion
  9.2 1.3 multiply_convert_fusion
  10.5 1.1 broadcast_in_dim.2
  11.6 3.7 %all-to-all-start = ((bf16[4,128,1024]{2,1,0:T(8,128)(2,1)}), bf16[4,128,1024]{2,1,0:T(8,128)(2,1)S(1)}, u32[]{:S(2)}, u32[]{:S(2)}) async-start(bf16[4,128,1024]{2,1,0:T(8,128)(2,1)} %bitcast.1), calls=%async_computation | async-start | bytes 2097152 | tf_op jit(solution)/shard_map/all_to_all | solution.py:123
  15.3 0.0 all-gather.2.cloned.1.call-start
  15.3 13.7 %all-to-all-done = bf16[4,128,1024]{2,1,0:T(8,128)(2,1)S(1)} async-done(((bf16[4,128,1024]{2,1,0:T(8,128)(2,1)}), bf16[4,128,1024]{2,1,0:T(8,128)(2,1)S(1)}, u32[]{:S(2)}, u32[]{:S(2)}) %all-to-all-start) | async-done | bytes 1048608 | tf_op jit(solution)/shard_map/all_to_all | solution.py:123
  29.0 2.7 %convolution_convert_fusion.v_ref = bf16[512,512]{1,0:T(8,128)(2,1)} fusion(bf16[512,1024]{1,0:T(8,128)(2,1)S(1)} %bitcast.32, bf16[1024,3072]{1,0:T(8,128)(2,1)} %param.7, s32[]{:T(128)S(6)} %select_n.11), kind=kOutput, calls=%fused_computation.12 | convolution fusion | flops 537133056 | bytes 2621444 | tf_op jit(solution)/shard_map/dot_general | solution.py:128
  31.8 2.7 %convolution_convert_fusion.1.k_ref = bf16[512,512]{1,0:T(8,128)(2,1)} fusion(bf16[512,1024]{1,0:T(8,128)(2,1)S(1)} %bitcast.33, bf16[1024,3072]{1,0:T(8,128)(2,1)} %param.7, s32[]{:T(128)S(6)} %select_n.10), kind=kOutput, calls=%fused_computation.13 | convolution fusion | flops 537133056 | bytes 2621444 | tf_op jit(solution)/shard_map/dot_general | solution.py:128
  34.5 2.7 %fusion.2.q_ref = bf16[512,512]{1,0:T(8,128)(2,1)} fusion(bf16[512,1024]{1,0:T(8,128)(2,1)S(1)} %bitcast.34, bf16[1024,3072]{1,0:T(8,128)(2,1)} %param.7, s32[]{:T(128)S(6)} %select_n.9), kind=kOutput, calls=%fused_computation.9 | convolution fusion | flops 537395200 | bytes 2621444 | tf_op jit(solution)/shard_map/dot_general | solution.py:128
  37.2 0.0 copy-start.2
  37.2 7.6 %frame_attention.1 = bf16[512,512]{1,0:T(8,128)(2,1)} custom-call(bf16[512,512]{1,0:T(8,128)(2,1)} %fusion.2.q_ref, bf16[512,512]{1,0:T(8,128)(2,1)} %convolution_convert_fusion.1.k_ref, bf16[512,512]{1,0:T(8,128)(2,1)} %convolution_convert_fusion.v_ref), custom_call_target="tpu_custom_call" | custom-call | tf_op jit(solution)/shard_map/frame_attention/pallas_call | solution.py:44
  44.8 11.5 %all_to_all.20 = bf16[4,128,512]{2,1,0:T(8,128)(2,1)S(1)} all-to-all(bf16[4,128,512]{2,1,0:T(8,128)(2,1)} %bitcast.31), channel_id=1, replica_groups=mesh['view'=8,'head'=4] {'head'}, dimensions={0} | all-to-all | bytes 1048576 | tf_op jit(solution)/shard_map/all_to_all | solution.py:135
  56.3 0.5 copy.12
  56.8 0.1 copy.15
  56.9 0.0 copy-done
  56.9 0.0 copy-done.2
  56.9 0.8 convert_reduce_fusion
  57.7 0.3 fusion.7
  58.0 6.3 %convolution_bitcast_fusion = f32[3072,256]{0,1:T(8,128)} fusion(bf16[1024,3072]{1,0:T(8,128)(2,1)} %param.9, bf16[256,1024]{1,0:T(8,128)(2,1)S(1)} %get-tuple-element.6, f32[256]{0:T(256)S(1)} %add_rsqrt_fusion, f32[256]{0:T(256)S(1)} %broadcast_multiply_fusion), kind=kOutput, calls=%fused_computation | convolution fusion | flops 1611661312 | bytes 9963520 | tf_op jit(solution)/shard_map/dot_general | solution.py:150
  64.4 0.0 copy-start.4
  64.4 3.6 %copy.13 = f32[3072,256]{1,0:T(8,128)} copy(f32[3072,256]{0,1:T(8,128)} %convolution_bitcast_fusion) | data formatting | bytes 6291456 | tf_op jit(solution)/shard_map/dot_general | solution.py:150
  68.0 0.0 copy-done.4
  68.0 2.3 %fusion.1 = bf16[16,3,64,256]{3,2,1,0:T(8,128)(2,1)S(1)} fusion(f32[3,16,64,256]{3,2,1,0:T(8,128)} %bitcast.26, f32[3]{0:T(128)S(1)} %copy-done.4), kind=kLoop, calls=%fused_computation.3 | loop fusion | flops 1572864 | bytes 4718604 | tf_op jit(solution)/shard_map/transpose | solution.py:154
  70.3 39.3 %all_to_all.21.q_ref = bf16[16,3,64,256]{3,2,1,0:T(8,128)(2,1)S(1)} all-to-all(bf16[16,3,64,256]{3,2,1,0:T(8,128)(2,1)S(1)} %fusion.1), channel_id=1, replica_groups={{0,1,2,3,8,9,10,11,16,17,18,19,24,25,26,27},{4,5,6,7,12,13,14,15,20,21,..., dimensions={0} | all-to-all | bytes 3145728 | tf_op jit(solution)/shard_map/all_to_all | solution.py:163
  109.6 0.0 copy-start.1
  109.6 1.1 copy-done.1
  110.7 1.0 slice.4
  111.8 0.0 all-gather.2.cloned.1.call-update
  111.8 11.0 %all-gather.2.cloned.1.call-done.kv_ref = bf16[32,2,64,256]{3,2,1,0:T(8,128)(2,1)} async-done(((bf16[16,2,64,256]{3,2,1,0:T(8,128)(2,1)}), bf16[32,2,64,256]{3,2,1,0:T(8,128)(2,1)}) %all-gather.2.cloned.1.call-update) | async-done | bytes 2097168 | tf_op jit(solution)/shard_map/all_gather | solution.py:166
  122.8 0.0 copy-start.3
  122.8 43.2 %global_attention.1 = bf16[16,64,256]{2,1,0:T(8,128)(2,1)} custom-call(bf16[16,3,64,256]{3,2,1,0:T(8,128)(2,1)} %copy-done.1, bf16[32,2,64,256]{3,2,1,0:T(8,128)(2,1)} %all-gather.2.cloned.1.call-done.kv_ref), custom_call_target="tpu_custom_call" | custom-call | tf_op jit(solution)/shard_map/global_attention/pallas_call | solution.py:96
  166.0 20.4 %all_to_all.22 = bf16[16,64,256]{2,1,0:T(8,128)(2,1)S(1)} all-to-all(bf16[16,64,256]{2,1,0:T(8,128)(2,1)} %global_attention.1), channel_id=1, replica_groups={{0,1,2,3,8,9,10,11,16,17,18,19,24,25,26,27},{4,5,6,7,12,13,14,15,20,21,..., dimensions={0} | all-to-all | bytes 1048576 | tf_op jit(solution)/shard_map/all_to_all | solution.py:177
  186.4 0.0 copy-done.3
  186.4 1.5 fusion.3
  (4 shorter events, 0.0 us)
Async XLA Ops:
  6.5 50.4 %copy-start = (bf16[1024,1024]{1,0:T(8,128)(2,1)S(1)}, bf16[1024,1024]{1,0:T(8,128)(2,1)}, u32[]{:S(2)}) copy-start(bf16[1024,1024]{1,0:T(8,128)(2,1)} %param.8) | copy-start | bytes 6291460
  11.6 17.4 %all-to-all-start = ((bf16[4,128,1024]{2,1,0:T(8,128)(2,1)}), bf16[4,128,1024]{2,1,0:T(8,128)(2,1)S(1)}, u32[]{:S(2)}, u32[]{:S(2)}) async-start(bf16[4,128,1024]{2,1,0:T(8,128)(2,1)} %bitcast.1), calls=%async_computation | async-start | bytes 2097152 | tf_op jit(solution)/shard_map/all_to_all | solution.py:123
  15.3 107.4 %all-gather.2.cloned.1.call-start = ((), (), s32[]{:S(2)}) async-start(), calls=%async_computation.4 | async-start | bytes 3145728 | tf_op jit(solution)/shard_map/all_gather | solution.py:166
  37.2 19.7 %copy-start.2 = (bf16[2,128,1024]{2,1,0:T(8,128)(2,1)S(1)}, bf16[2,128,1024]{2,1,0:T(8,128)(2,1)}, u32[]{:S(2)}) copy-start(bf16[2,128,1024]{2,1,0:T(8,128)(2,1)} %param.6) | copy-start | bytes 1572868
  64.4 3.6 %copy-start.4 = (f32[3]{0:T(128)S(1)}, f32[3]{0:T(128)}, u32[]{:S(2)}) copy-start(f32[3]{0:T(128)} %constant.38.clone) | copy-start | bytes 40
  109.6 1.1 copy-start.1
  122.8 63.6 %copy-start.3 = (bf16[1024,1024]{1,0:T(8,128)(2,1)S(1)}, bf16[1024,1024]{1,0:T(8,128)(2,1)}, u32[]{:S(2)}) copy-start(bf16[1024,1024]{1,0:T(8,128)(2,1)} %param.10) | copy-start | bytes 6291460
Sparse Core Ops, SparseCore 0:
  111.9 10.7 all-gather.1

commit v2 on v1

--- a/solution.py
+++ b/solution.py
@@ -52,63 +52,234 @@
     )(queries, keys, values)
 
 
-def global_kernel(key_step, q_ref, kv_ref, o_ref, keys, values):
-    pieces, _, head, width = kv_ref.shape
-
-    @pl.when(pl.program_id(0) == 0)
-    def _():
-        def lay_out(piece, carry):
-            at = pl.ds(pl.multiple_of(piece * width, width), width)
-            keys[:, at] = kv_ref[piece, 0]
-            wide = jnp.concatenate(
-                [kv_ref[piece, 1], jnp.ones((LANES - head, width), jnp.bfloat16)], axis=0
+def global_kernel(
+    planes, copies, per_plane, key_step,
+    packed, out_ref,
+    got_q, got_kv, keys, values, peaks, accums, out_buf,
+    q_send, q_recv, kv_send, kv_recv, on_send, on_recv, out_send, out_recv,
+):
+    _, _, head, width = packed.shape
+    view, spot = lax.axis_index("view"), lax.axis_index("head")
+    plane, copy = view // copies, lax.rem(view, copies)
+    mine = plane * per_plane + spot
+    stage_rows = per_plane * width
+
+    def device(to_plane, to_copy, to_spot):
+        return (to_plane * copies + to_copy, to_spot)
+
+    def remote(src, dst, send, recv, target):
+        return pltpu.make_async_remote_copy(
+            src_ref=src, dst_ref=dst, send_sem=send, recv_sem=recv,
+            device_id=target, device_id_type=pl.DeviceIdType.MESH,
+        )
+
+    def q_copy(stage, step):
+        to_plane, to_spot = lax.rem(plane + stage, planes), lax.rem(spot + step, per_plane)
+        slot, order = stage * per_plane + spot, stage * per_plane + step
+        return remote(
+            packed.at[to_plane * per_plane + to_spot, 0], got_q.at[slot],
+            q_send.at[order], q_recv.at[slot], device(to_plane, copy, to_spot),
+        )
+
+    def kv_copy(stage, step):
+        to_plane, to_spot = lax.rem(plane + stage, planes), lax.rem(spot + step, per_plane)
+        slot, order = stage * per_plane + spot, stage * per_plane + step
+        return remote(
+            packed.at[to_plane * per_plane + to_spot, pl.ds(1, 2)], got_kv.at[0, slot],
+            kv_send.at[order], kv_recv.at[slot], device(to_plane, copy, to_spot),
+        )
+
+    def on_copy(slot, hop):
+        return remote(
+            got_kv.at[0, slot], got_kv.at[hop, slot], on_send.at[hop - 1, slot],
+            on_recv.at[hop - 1, slot], device(plane, lax.rem(copy + hop, copies), spot),
+        )
+
+    def back_copy(slot, stage, to_spot):
+        return remote(
+            out_buf.at[slot], out_ref.at[mine], out_send.at[slot], out_recv.at[mine],
+            device(lax.rem(plane + planes - stage, planes), copy, to_spot),
+        )
+
+    def back_own():
+        return pltpu.make_async_copy(out_buf.at[spot], out_ref.at[mine], out_recv.at[mine])
+
+    def arrive(ref, sem):
+        pltpu.make_async_copy(ref, ref, sem).wait()
+
+    barrier = pltpu.get_barrier_semaphore()
+    partners = [
+        device(lax.rem(plane + stage, planes), copy, lax.rem(spot + step, per_plane))
+        for stage in range(planes)
+        for step in range(per_plane)
+        if stage or step
+    ] + [device(plane, lax.rem(copy + hop, copies), spot) for hop in range(1, copies)]
+    for partner in partners:
+        pl.semaphore_signal(
+            barrier, inc=1, device_id=partner, device_id_type=pl.DeviceIdType.MESH
+        )
+    pltpu.make_async_copy(packed.at[mine, 0], got_q.at[spot], q_recv.at[spot]).start()
+    pltpu.make_async_copy(
+        packed.at[mine, pl.ds(1, 2)], got_kv.at[0, spot], kv_recv.at[spot]
+    ).start()
+    peaks[...] = jnp.full_like(peaks, -1e30)
+    accums[...] = jnp.zeros_like(accums)
+    pl.semaphore_wait(barrier, len(partners))
+
+    def start_stage(make, stage):
+        for step in range(per_plane):
+            if stage or step:
+                make(stage, step).start()
+
+    start_stage(kv_copy, 0)
+    start_stage(q_copy, 0)
+    for stage in range(1, planes):
+        start_stage(q_copy, stage)
+    for stage in range(1, planes):
+        start_stage(kv_copy, stage)
+
+    def hand_on(stage):
+        for i in range(per_plane):
+            slot = stage * per_plane + i
+            arrive(got_kv.at[0, slot], kv_recv.at[slot])
+            for hop in range(1, copies):
+                on_copy(slot, hop).start()
+
+    def send_back(stage):
+        for i in range(per_plane):
+            slot = stage * per_plane + i
+            own = jnp.logical_and(stage == 0, spot == i)
+
+            @pl.when(own)
+            def _():
+                back_own().start()
+
+            @pl.when(jnp.logical_not(own))
+            def _():
+                back_copy(slot, stage, i).start()
+
+    hand_on(0)
+
+    def step_fn(step, carry):
+        stage, turn = step // planes, lax.rem(step, planes)
+        last = (stage + 1) // planes
+        block = turn + last * (planes - 1 - 2 * turn)
+
+        @pl.when(turn == 0)
+        def _():
+            for hop in range(1, copies):
+                for i in range(per_plane):
+                    slot = stage * per_plane + i
+                    arrive(got_kv.at[hop, slot], on_recv.at[hop - 1, slot])
+            for hop in range(copies):
+                for i in range(per_plane):
+                    slot = stage * per_plane + i
+                    at = (hop * per_plane + i) * width
+                    keys[:, at : at + width] = got_kv[hop, slot, 0]
+                    wide = jnp.concatenate(
+                        [
+                            got_kv[hop, slot, 1],
+                            jnp.ones((LANES - head, width), jnp.bfloat16),
+                        ],
+                        axis=0,
+                    )
+                    values[at : at + width, :] = wide.T
+
+        @pl.when(stage == 0)
+        def _():
+            for i in range(per_plane):
+                slot = block * per_plane + i
+                arrive(got_q.at[slot], q_recv.at[slot])
+
+        @pl.when(jnp.logical_and(turn == planes - 1, last == 0))
+        def _():
+            hand_on(stage + 1)
+
+        @pl.when(jnp.logical_and(turn > 0, last == 1))
+        def _():
+            send_back(block + 1)
+
+        queries = jnp.concatenate(
+            [got_q[block * per_plane + i] for i in range(per_plane)], axis=1
+        ).T
+        rows = pl.ds(pl.multiple_of(block * stage_rows, stage_rows), stage_rows)
+        peak, accum = peaks[rows, :], accums[rows, :]
+        for start in range(0, copies * stage_rows, key_step):
+            scores = jnp.dot(
+                queries, keys[:, start : start + key_step], preferred_element_type=jnp.float32
             )
-            values[at, :] = wide.T
-            return carry
-
-        lax.fori_loop(0, pieces, lay_out, 0)
-
-    blocks = q_ref.shape[0]
-    queries = jnp.concatenate([q_ref[i, 0] for i in range(blocks)], axis=1).T
-    rows = queries.shape[0]
-    peak = jnp.full((rows, 1), -1e30, jnp.float32)
-    accum = jnp.zeros((rows, LANES), jnp.float32)
-    for start in range(0, pieces * width, key_step):
-        scores = jnp.dot(
-            queries, keys[:, start : start + key_step], preferred_element_type=jnp.float32
-        )
-        peak_new = jnp.maximum(peak, jnp.max(scores, axis=1, keepdims=True))
-        terms = jnp.exp2(scores - peak_new).astype(jnp.bfloat16)
-        accum = accum * jnp.exp2(peak - peak_new) + jnp.dot(
-            terms, values[start : start + key_step, :], preferred_element_type=jnp.float32
-        )
-        peak = peak_new
-    mixed = (accum[:, :head] / accum[:, head : head + 1]).T.astype(jnp.bfloat16)
-    for i in range(blocks):
-        o_ref[i] = mixed[:, i * width : (i + 1) * width]
-
-
-def global_attention(packed, key_values, query_step, key_step):
-    sources, _, head, width = packed.shape
-    pieces = key_values.shape[0]
-    blocks = min(sources, max(1, query_step // width))
-    key_step = min(key_step, pieces * width)
+            peak_new = jnp.maximum(peak, jnp.max(scores, axis=1, keepdims=True))
+            terms = jnp.exp2(scores - peak_new).astype(jnp.bfloat16)
+            accum = accum * jnp.exp2(peak - peak_new) + jnp.dot(
+                terms, values[start : start + key_step, :], preferred_element_type=jnp.float32
+            )
+            peak = peak_new
+        peaks[rows, :] = peak
+        accums[rows, :] = accum
+
+        @pl.when(last == 1)
+        def _():
+            total = accums[rows, :]
+            mixed = (total[:, :head] / total[:, head : head + 1]).T.astype(jnp.bfloat16)
+            for i in range(per_plane):
+                out_buf[block * per_plane + i] = mixed[:, i * width : (i + 1) * width]
+
+        return carry
+
+    lax.fori_loop(0, planes * planes, step_fn, 0)
+
+    for stage in range(planes):
+        for step in range(per_plane):
+            if stage or step:
+                q_copy(stage, step).wait_send()
+                kv_copy(stage, step).wait_send()
+    send_back(0)
+    for slot in range(planes * per_plane):
+        for hop in range(1, copies):
+            on_copy(slot, hop).wait_send()
+    for stage in range(planes):
+        for i in range(per_plane):
+            slot = stage * per_plane + i
+            if stage:
+                back_copy(slot, stage, i).wait_send()
+            else:
+
+                @pl.when(spot != i)
+                def _():
+                    back_copy(slot, stage, i).wait_send()
+
+    for slot in range(planes * per_plane):
+        arrive(out_ref.at[slot], out_recv.at[slot])
+
+
+def global_attention(packed, planes, copies, per_plane, key_step):
+    heads, _, head, width = packed.shape
+    stage_rows = per_plane * width
+    rows = planes * stage_rows
+    key_step = min(key_step, stage_rows)
+    dma = pltpu.SemaphoreType.DMA
+    hops = max(1, copies - 1)
     return pl.pallas_call(
-        functools.partial(global_kernel, key_step),
-        grid=(sources // blocks,),
-        in_specs=[
-            pl.BlockSpec((blocks, 1, head, width), lambda i: (i, 0, 0, 0)),
-            pl.BlockSpec((pieces, 2, head, width), lambda i: (0, 0, 0, 0)),
+        functools.partial(global_kernel, planes, copies, per_plane, key_step),
+        in_specs=[pl.BlockSpec(memory_space=pl.ANY)],
+        out_specs=pl.BlockSpec(memory_space=pltpu.VMEM),
+        out_shape=jax.ShapeDtypeStruct((heads, head, width), jnp.bfloat16),
+        scratch_shapes=[
+            pltpu.VMEM((heads, head, width), jnp.bfloat16),
+            pltpu.VMEM((copies, heads, 2, head, width), jnp.bfloat16),
+            pltpu.VMEM((head, copies * stage_rows), jnp.bfloat16),
+            pltpu.VMEM((copies * stage_rows, LANES), jnp.bfloat16),
+            pltpu.VMEM((rows, 1), jnp.float32),
+            pltpu.VMEM((rows, LANES), jnp.float32),
+            pltpu.VMEM((heads, head, width), jnp.bfloat16),
+            dma((heads,)), dma((heads,)), dma((heads,)), dma((heads,)),
+            dma((hops, heads)), dma((hops, heads)), dma((heads,)), dma((heads,)),
         ],
-        out_specs=pl.BlockSpec((blocks, head, width), lambda i: (i, 0, 0)),
-        out_shape=jax.ShapeDtypeStruct((sources, head, width), jnp.bfloat16),
-        scratch_shapes=[
-            pltpu.VMEM((head, pieces * width), jnp.bfloat16),
-            pltpu.VMEM((pieces * width, LANES), jnp.bfloat16),
-        ],
-        compiler_params=pltpu.CompilerParams(vmem_limit_bytes=VMEM_BYTES),
+        compiler_params=pltpu.CompilerParams(
+            collective_id=0, has_side_effects=True, vmem_limit_bytes=VMEM_BYTES
+        ),
         name="global_attention",
-    )(packed, key_values)
+    )(packed)
 
 
 def on_device(tokens, w_qkv_frame, w_out_frame, w_qkv_global, w_out_global):
@@ -152,30 +323,8 @@
     ).reshape(3, heads, HEAD, tokens_here)
     scale = jnp.array([SCORE_SCALE, 1.0, 1.0], jnp.float32).reshape(3, 1, 1, 1)
     packed = jnp.transpose((packed * scale).astype(jnp.bfloat16), (1, 0, 2, 3))
-    groups = [
-        [
-            (outer * copies + copy) * head_size + inner
-            for outer in range(view_size // copies)
-            for inner in range(head_size)
-        ]
-        for copy in range(copies)
-    ]
-    by_head = lax.all_to_all(
-        packed, ("view", "head"), split_axis=0, concat_axis=0, axis_index_groups=groups, tiled=True
-    )
-    key_values = lax.all_gather(
-        by_head[:, 1:],
-        "view",
-        axis=0,
-        axis_index_groups=[
-            [outer * copies + copy for copy in range(copies)]
-            for outer in range(view_size // copies)
-        ],
-        tiled=True,
-    )
-    mixed = global_attention(by_head, key_values, 1024, 1024)
-    mixed = lax.all_to_all(
-        mixed, ("view", "head"), split_axis=0, concat_axis=0, axis_index_groups=groups, tiled=True
+    mixed = global_attention(
+        packed, view_size // copies, copies, head_size, 1024
     ).reshape(model_dim, tokens_here)
     added = lax.dot_general(
         mixed, w_out_global, (((0,), (0,)), ((), ())), preferred_element_type=jnp.float32

time: 199 us -> 161 us (0.81); the launches traced: 195 us -> 160 us
  blocking collectives: 71.2 us -> 11.5 us
  Pallas kernels: 50.8 us -> 100 us
  between operations: 13.5 us -> 0.08 us
  waiting for transfers between devices: 24.7 us -> 13.7 us
  local copies, waits for them, and re-layouts: 7.52 us -> 5.31 us
    all_to_all x2 -> x0, blocking collectives: 59.7 us -> none  [the longest x1 39.3 us: on_device(): lax.all_to_all(packed, ('view', 'head'), split_axis=0, concat_axis=0, axi...]
    pallas_call x1, Pallas kernels: 43.2 us -> 92.6 us  [global_attention(): pl.pallas_call(functools.partial(global_kernel, planes, copies, per_plane...]
    all_gather x1 -> x0, waiting for transfers between devices: 11 us -> none  [on_device(): lax.all_gather(by_head[:, 1:], 'view', axis=0, axis_index_groups=[[outer...]
  transfers between devices with their start and end apart: 2 -> 1, of which waited for: 2 -> 1; matrix products, arithmetic and copies ran while one was open for 0% -> 0% of each run, Pallas kernels for 0% -> 0%
where the time goes in v2:
time: 161 us; the launch traced here: 160 us
  Pallas kernels  100 us (62%)
  matrix products  17.9 us (11%)
  waiting for transfers between devices  13.7 us (9%)
  blocking collectives  11.5 us (7%)
  other arithmetic  7.86 us (5%)
  local copies, waits for them, and re-layouts  5.31 us (3%)
  starting transfers between devices  3.72 us (2%)
    pallas_call x1, Pallas kernels, global_attention(): pl.pallas_call(functools.partial(global_kernel, planes, copies, per_plane...  92.6 us
    all_to_all x1, waiting for transfers between devices, on_device(): lax.all_to_all(sent, 'head', split_axis=0, concat_axis=0, tiled=True)  13.7 us
    all_to_all x1, blocking collectives, on_device(): lax.all_to_all(frame_mixed.reshape(head_size, rows_here, cols), 'head', s...  11.5 us
    dot_general x3, matrix products, project(): return jnp.dot(view_rows, weight, preferred_element_type=jnp.float32)  8.21 us
    pallas_call x1, Pallas kernels, frame_attention(): pl.pallas_call(frame_kernel, grid=(cols // LANES,), in_specs=[spec] * 3,...  7.56 us
    dot_general x1, matrix products, on_device(): lax.dot_general(w_qkv_global, normed, (((0,), (1,)), ((), ())), preferred...  6.38 us
    all_to_all x1, starting transfers between devices, on_device(): lax.all_to_all(sent, 'head', split_axis=0, concat_axis=0, tiled=True)  3.72 us
    transpose x1, other arithmetic, on_device(): packed = jnp.transpose((packed * scale).astype(jnp.bfloat16), (1, 0, 2, 3))  3.61 us
  transfers between devices with their start and end apart: 1, of which 1 were waited for; matrix products, arithmetic and copies ran while one was open for 0% of the time, Pallas kernels for 0%

profile of v2, /device:TPU:16, one launch (start us, length us, event | category | flops | bytes accessed | tf_op | source)
XLA Modules:
  0.0 160.2 jit_solution(15304235126032296583)
XLA Ops:
  0.0 0.0 copy-start
  0.0 1.3 convert_reduce_fusion.1
  1.3 1.3 multiply_reduce_fusion
  2.7 1.3 multiply_convert_fusion
  4.0 1.1 broadcast_in_dim.2
  5.1 3.7 %all-to-all-start = ((bf16[4,128,1024]{2,1,0:T(8,128)(2,1)}), bf16[4,128,1024]{2,1,0:T(8,128)(2,1)S(1)}, u32[]{:S(2)}, u32[]{:S(2)}) async-start(bf16[4,128,1024]{2,1,0:T(8,128)(2,1)} %bitcast.1), calls=%async_computation | async-start | bytes 2097152 | tf_op jit(solution)/shard_map/all_to_all | solution.py:294
  8.8 13.7 %all-to-all-done = bf16[4,128,1024]{2,1,0:T(8,128)(2,1)S(1)} async-done(((bf16[4,128,1024]{2,1,0:T(8,128)(2,1)}), bf16[4,128,1024]{2,1,0:T(8,128)(2,1)S(1)}, u32[]{:S(2)}, u32[]{:S(2)}) %all-to-all-start) | async-done | bytes 1048608 | tf_op jit(solution)/shard_map/all_to_all | solution.py:294
  22.5 2.7 %convolution_convert_fusion.v_ref = bf16[512,512]{1,0:T(8,128)(2,1)} fusion(bf16[512,1024]{1,0:T(8,128)(2,1)S(1)} %bitcast.32, bf16[1024,3072]{1,0:T(8,128)(2,1)} %param.7, s32[]{:T(128)S(6)} %select_n.11), kind=kOutput, calls=%fused_computation.12 | convolution fusion | flops 537133056 | bytes 2621444 | tf_op jit(solution)/shard_map/dot_general | solution.py:299
  25.2 2.7 %convolution_convert_fusion.1.k_ref = bf16[512,512]{1,0:T(8,128)(2,1)} fusion(bf16[512,1024]{1,0:T(8,128)(2,1)S(1)} %bitcast.33, bf16[1024,3072]{1,0:T(8,128)(2,1)} %param.7, s32[]{:T(128)S(6)} %select_n.10), kind=kOutput, calls=%fused_computation.13 | convolution fusion | flops 537133056 | bytes 2621444 | tf_op jit(solution)/shard_map/dot_general | solution.py:299
  28.0 2.7 %fusion.2.q_ref = bf16[512,512]{1,0:T(8,128)(2,1)} fusion(bf16[512,1024]{1,0:T(8,128)(2,1)S(1)} %bitcast.34, bf16[1024,3072]{1,0:T(8,128)(2,1)} %param.7, s32[]{:T(128)S(6)} %select_n.9), kind=kOutput, calls=%fused_computation.9 | convolution fusion | flops 537395200 | bytes 2621444 | tf_op jit(solution)/shard_map/dot_general | solution.py:299
  30.7 0.0 copy-start.1
  30.7 7.6 %frame_attention.1 = bf16[512,512]{1,0:T(8,128)(2,1)} custom-call(bf16[512,512]{1,0:T(8,128)(2,1)} %fusion.2.q_ref, bf16[512,512]{1,0:T(8,128)(2,1)} %convolution_convert_fusion.1.k_ref, bf16[512,512]{1,0:T(8,128)(2,1)} %convolution_convert_fusion.v_ref), custom_call_target="tpu_custom_call" | custom-call | tf_op jit(solution)/shard_map/frame_attention/pallas_call | solution.py:44
  38.3 11.5 %all_to_all.10 = bf16[4,128,512]{2,1,0:T(8,128)(2,1)S(1)} all-to-all(bf16[4,128,512]{2,1,0:T(8,128)(2,1)} %bitcast.31), channel_id=1, replica_groups=mesh['view'=8,'head'=4] {'head'}, dimensions={0} | all-to-all | bytes 1048576 | tf_op jit(solution)/shard_map/all_to_all | solution.py:306
  49.7 0.5 copy.9
  50.3 0.1 copy.12
  50.3 0.0 copy-done
  50.4 0.0 copy-done.1
  50.4 0.8 convert_reduce_fusion
  51.2 0.3 fusion.7
  51.5 6.4 %convolution_bitcast_fusion = f32[3072,256]{0,1:T(8,128)} fusion(bf16[1024,3072]{1,0:T(8,128)(2,1)} %param.9, bf16[256,1024]{1,0:T(8,128)(2,1)S(1)} %get-tuple-element.6, f32[256]{0:T(256)S(1)} %add_rsqrt_fusion, f32[256]{0:T(256)S(1)} %broadcast_multiply_fusion), kind=kOutput, calls=%fused_computation | convolution fusion | flops 1611661312 | bytes 9963520 | tf_op jit(solution)/shard_map/dot_general | solution.py:321
  57.9 0.0 copy-start.3
  57.9 3.6 %copy.10 = f32[3072,256]{1,0:T(8,128)} copy(f32[3072,256]{0,1:T(8,128)} %convolution_bitcast_fusion) | data formatting | bytes 6291456 | tf_op jit(solution)/shard_map/dot_general | solution.py:321
  61.4 0.0 copy-done.3
  61.4 0.0 copy-start.2
  61.4 3.6 %fusion.1.packed = bf16[16,3,64,256]{3,2,1,0:T(8,128)(2,1)} fusion(f32[3,16,64,256]{3,2,1,0:T(8,128)} %bitcast.26, f32[3]{0:T(128)S(1)} %copy-done.3), kind=kLoop, calls=%fused_computation.3 | loop fusion | flops 1572864 | bytes 4718604 | tf_op jit(solution)/shard_map/transpose | solution.py:325
  65.0 92.6 %global_attention.1 = bf16[16,64,256]{2,1,0:T(8,128)(2,1)} custom-call(bf16[16,3,64,256]{3,2,1,0:T(8,128)(2,1)} %fusion.1.packed), custom_call_target="tpu_custom_call" | custom-call | tf_op jit(solution)/shard_map/global_attention/pallas_call | solution.py:262
  157.6 0.0 copy-done.2
  157.6 2.6 %fusion.3 = bf16[256,1024]{1,0:T(8,128)(2,1)} fusion(bf16[1024,256]{1,0:T(8,128)(2,1)} %bitcast.28, bf16[1024,1024]{1,0:T(8,128)(2,1)S(1)} %copy-done.2, bf16[256,1024]{1,0:T(8,128)(2,1)S(1)} %get-tuple-element.6), kind=kOutput, calls=%fused_computation.10 | convolution fusion | flops 537657344 | bytes 3670016 | tf_op jit(solution)/shard_map/dot_general | solution.py:329
  (4 shorter events, 0.0 us)
Async XLA Ops:
  0.0 50.3 %copy-start = (bf16[1024,1024]{1,0:T(8,128)(2,1)S(1)}, bf16[1024,1024]{1,0:T(8,128)(2,1)}, u32[]{:S(2)}) copy-start(bf16[1024,1024]{1,0:T(8,128)(2,1)} %param.8) | copy-start | bytes 6291460
  5.1 17.4 %all-to-all-start = ((bf16[4,128,1024]{2,1,0:T(8,128)(2,1)}), bf16[4,128,1024]{2,1,0:T(8,128)(2,1)S(1)}, u32[]{:S(2)}, u32[]{:S(2)}) async-start(bf16[4,128,1024]{2,1,0:T(8,128)(2,1)} %bitcast.1), calls=%async_computation | async-start | bytes 2097152 | tf_op jit(solution)/shard_map/all_to_all | solution.py:294
  30.7 19.7 %copy-start.1 = (bf16[2,128,1024]{2,1,0:T(8,128)(2,1)S(1)}, bf16[2,128,1024]{2,1,0:T(8,128)(2,1)}, u32[]{:S(2)}) copy-start(bf16[2,128,1024]{2,1,0:T(8,128)(2,1)} %param.6) | copy-start | bytes 1572868
  57.9 3.6 %copy-start.3 = (f32[3]{0:T(128)S(1)}, f32[3]{0:T(128)}, u32[]{:S(2)}) copy-start(f32[3]{0:T(128)} %constant.38.clone) | copy-start | bytes 40
  61.4 96.2 %copy-start.2 = (bf16[1024,1024]{1,0:T(8,128)(2,1)S(1)}, bf16[1024,1024]{1,0:T(8,128)(2,1)}, u32[]{:S(2)}) copy-start(bf16[1024,1024]{1,0:T(8,128)(2,1)} %param.10) | copy-start | bytes 6291460

commit v3 on v2

--- a/solution.py
+++ b/solution.py
@@ -21,35 +21,209 @@
     return ((widened - center) * lax.rsqrt(spread + 1e-06)).astype(jnp.bfloat16)
 
 
-def frame_kernel(q_ref, k_ref, v_ref, o_ref):
-    outs = []
-    for head in range(q_ref.shape[1] // HEAD):
-        cols = slice(head * HEAD, (head + 1) * HEAD)
-        scores = lax.dot_general(
-            q_ref[:, cols], k_ref[:, cols], (((1,), (1,)), ((), ())),
-            preferred_element_type=jnp.float32,
-        )
-        terms = jnp.exp2(scores - jnp.max(scores, axis=1, keepdims=True))
-        total = jnp.sum(terms, axis=1, keepdims=True)
-        mixed = jnp.dot(
-            terms.astype(jnp.bfloat16), v_ref[:, cols], preferred_element_type=jnp.float32
-        )
-        outs.append(mixed / total)
-    o_ref[...] = jnp.concatenate(outs, axis=1).astype(jnp.bfloat16)
-
-
-def frame_attention(queries, keys, values):
-    rows, cols = queries.shape
-    spec = pl.BlockSpec((rows, LANES), lambda i: (0, i))
+def frame_kernel(
+    shares, tokens_ref, weight_ref, back_ref,
+    sent, got, weights, packed, out_buf,
+    weight_sem, token_send, token_recv, out_send, out_recv,
+):
+    spots, rows, model_dim = got.shape
+    cols = weights.shape[2]
+    pairs = cols // LANES
+    view, spot = lax.axis_index("view"), lax.axis_index("head")
+    share = lax.rem(spot, shares)
+
+    def remote(src, dst, send, recv, to_spot):
+        return pltpu.make_async_remote_copy(
+            src_ref=src, dst_ref=dst, send_sem=send, recv_sem=recv,
+            device_id=(view, to_spot), device_id_type=pl.DeviceIdType.MESH,
+        )
+
+    def weight_copy(which):
+        at = pl.multiple_of(which * model_dim + share * cols, LANES)
+        return pltpu.make_async_copy(
+            weight_ref.at[:, pl.ds(at, cols)], weights.at[which], weight_sem.at[which]
+        )
+
+    def token_copy(step):
+        to_spot = lax.rem(spot + step, spots)
+        return remote(
+            sent.at[to_spot // shares], got.at[spot], token_send.at[step],
+            token_recv.at[spot], to_spot,
+        )
+
+    def token_own():
+        return pltpu.make_async_copy(sent.at[spot // shares], got.at[spot], token_recv.at[spot])
+
+    def out_copy(pair, step):
+        to_spot = lax.rem(spot + step, spots)
+        return remote(
+            out_buf.at[to_spot, pair], back_ref.at[spot, pair], out_send.at[pair, step],
+            out_recv.at[pair, spot], to_spot,
+        )
+
+    def out_own(pair):
+        return pltpu.make_async_copy(
+            out_buf.at[spot, pair], back_ref.at[spot, pair], out_recv.at[pair, spot]
+        )
+
+    def arrive(ref, sem):
+        pltpu.make_async_copy(ref, ref, sem).wait()
+
+    for which in range(3):
+        weight_copy(which).start()
+    sent[...] = normalize(tokens_ref[...])
+    barrier = pltpu.get_barrier_semaphore()
+    for step in range(1, spots):
+        pl.semaphore_signal(
+            barrier, inc=1, device_id=(view, lax.rem(spot + step, spots)),
+            device_id_type=pl.DeviceIdType.MESH,
+        )
+    pl.semaphore_wait(barrier, spots - 1)
+    for step in range(1, spots):
+        token_copy(step).start()
+    token_own().start()
+    for which in range(3):
+        weight_copy(which).wait()
+
+    def project(step, carry):
+        source = lax.rem(spot + spots - step, spots)
+        arrive(got.at[source], token_recv.at[source])
+        at = pl.ds(pl.multiple_of(source * rows, rows), rows)
+        for which in range(3):
+            part = jnp.dot(got[source], weights[which], preferred_element_type=jnp.float32)
+            if which == 0:
+                part = part * SCORE_SCALE
+            packed[which, at, :] = part.astype(jnp.bfloat16)
+        return carry
+
+    lax.fori_loop(0, spots, project, 0)
+
+    def send_pair(pair):
+        for step in range(1, spots):
+            out_copy(pair, step).start()
+        out_own(pair).start()
+
+    low = lax.broadcasted_iota(jnp.int32, (spots * rows, LANES), 1) < HEAD
+    for pair in range(pairs):
+        at = slice(pair * LANES, (pair + 1) * LANES)
+        queries, keys, values = packed[0, :, at], packed[1, :, at], packed[2, :, at]
+        outs = []
+        for mask in (low, jnp.logical_not(low)):
+            scores = lax.dot_general(
+                queries, jnp.where(mask, keys, 0), (((1,), (1,)), ((), ())),
+                preferred_element_type=jnp.float32,
+            )
+            terms = jnp.exp2(scores - jnp.max(scores, axis=1, keepdims=True))
+            outs.append(
+                jnp.dot(
+                    terms.astype(jnp.bfloat16), jnp.where(mask, values, 1),
+                    preferred_element_type=jnp.float32,
+                )
+            )
+        total = jnp.where(low, outs[0][:, LANES - 1 :], outs[1][:, :1])
+        mixed = (jnp.where(low, outs[0], outs[1]) / total).astype(jnp.bfloat16)
+        for i in range(spots):
+            out_buf[i, pair] = mixed[i * rows : (i + 1) * rows]
+        if pair:
+            send_pair(pair - 1)
+    for step in range(1, spots):
+        token_copy(step).wait_send()
+    send_pair(pairs - 1)
+    for pair in range(pairs):
+        for step in range(1, spots):
+            out_copy(pair, step).wait_send()
+        for i in range(spots):
+            arrive(back_ref.at[i, pair], out_recv.at[pair, i])
+
+
+def frame_attention(tokens, weight, spots):
+    views, rows, model_dim = tokens.shape
+    shares = spots // views
+    cols = model_dim // shares
+    pairs = cols // LANES
+    dma = pltpu.SemaphoreType.DMA
     return pl.pallas_call(
-        frame_kernel,
-        grid=(cols // LANES,),
-        in_specs=[spec] * 3,
-        out_specs=spec,
-        out_shape=jax.ShapeDtypeStruct((rows, cols), jnp.bfloat16),
+        functools.partial(frame_kernel, shares),
+        in_specs=[
+            pl.BlockSpec(memory_space=pltpu.VMEM),
+            pl.BlockSpec(memory_space=pl.ANY),
+        ],
+        out_specs=pl.BlockSpec(memory_space=pltpu.VMEM),
+        out_shape=jax.ShapeDtypeStruct((spots, pairs, rows, LANES), jnp.bfloat16),
+        scratch_shapes=[
+            pltpu.VMEM((views, rows, model_dim), jnp.bfloat16),
+            pltpu.VMEM((spots, rows, model_dim), jnp.bfloat16),
+            pltpu.VMEM((3, model_dim, cols), jnp.bfloat16),
+            pltpu.VMEM((3, spots * rows, cols), jnp.bfloat16),
+            pltpu.VMEM((spots, pairs, rows, LANES), jnp.bfloat16),
+            dma((3,)), dma((spots,)), dma((spots,)),
+            dma((pairs, spots)), dma((pairs, spots)),
+        ],
+        compiler_params=pltpu.CompilerParams(
+            collective_id=1, has_side_effects=True, vmem_limit_bytes=VMEM_BYTES
+        ),
+        name="frame_attention",
+    )(tokens, weight)
+
+
+def project_kernel(
+    query_blocks, tokens_ref, back_ref, w_out_ref, w_qkv_ref, after_ref, packed_ref, normed
+):
+    views, rows, model_dim = tokens_ref.shape
+    spots, pairs, _, _ = back_ref.shape
+    shares = spots // views
+
+    @pl.when(pl.program_id(0) == 0)
+    def _():
+        mixed = jnp.concatenate(
+            [
+                jnp.concatenate(
+                    [
+                        back_ref[view * shares + share, pair]
+                        for share in range(shares)
+                        for pair in range(pairs)
+                    ],
+                    axis=1,
+                )
+                for view in range(views)
+            ],
+            axis=0,
+        )
+        added = jnp.dot(mixed, w_out_ref[...], preferred_element_type=jnp.float32)
+        stream = tokens_ref[...].reshape(views * rows, model_dim).astype(jnp.float32)
+        after = (stream + added).astype(jnp.bfloat16)
+        after_ref[...] = after
+        normed[...] = normalize(after)
+
+    part = jnp.dot(normed[...], w_qkv_ref[...], preferred_element_type=jnp.float32)
+    part = part * jnp.where(pl.program_id(0) < query_blocks, SCORE_SCALE, 1.0)
+    part = part.astype(jnp.bfloat16).T
+    for i in range(packed_ref.shape[0]):
+        packed_ref[i, 0] = part[i * HEAD : (i + 1) * HEAD]
+
+
+def project_global(tokens, back, w_out, w_qkv):
+    views, rows, model_dim = tokens.shape
+    tokens_here = views * rows
+    block = 4 * HEAD
+    blocks = model_dim // block
+    whole = pl.BlockSpec(memory_space=pltpu.VMEM)
+    return pl.pallas_call(
+        functools.partial(project_kernel, blocks),
+        grid=(3 * blocks,),
+        in_specs=[whole, whole, whole, pl.BlockSpec((model_dim, block), lambda i: (0, i))],
+        out_specs=[
+            whole,
+            pl.BlockSpec((4, 1, HEAD, tokens_here), lambda i: (i % blocks, i // blocks, 0, 0)),
+        ],
+        out_shape=[
+            jax.ShapeDtypeStruct((tokens_here, model_dim), jnp.bfloat16),
+            jax.ShapeDtypeStruct((model_dim // HEAD, 3, HEAD, tokens_here), jnp.bfloat16),
+        ],
+        scratch_shapes=[pltpu.VMEM((tokens_here, model_dim), jnp.bfloat16)],
         compiler_params=pltpu.CompilerParams(vmem_limit_bytes=VMEM_BYTES),
-        name="frame_attention",
-    )(queries, keys, values)
+        name="project_global",
+    )(tokens, back, w_out, w_qkv)
 
 
 def global_kernel(
@@ -287,42 +461,10 @@
     head_size, view_size = lax.axis_size("head"), lax.axis_size("view")
     tokens_here = view_here * rows_here
 
-    shares = head_size // view_here
-    cols = model_dim // shares
-    share = lax.rem(lax.axis_index("head"), shares)
-    sent = jnp.repeat(normalize(tokens), shares, axis=0)
-    view_rows = lax.all_to_all(sent, "head", split_axis=0, concat_axis=0, tiled=True)
-    view_rows = view_rows.reshape(head_size * rows_here, model_dim)
-
-    def project(which):
-        weight = lax.dynamic_slice_in_dim(w_qkv_frame, which * model_dim + share * cols, cols, 1)
-        return jnp.dot(view_rows, weight, preferred_element_type=jnp.float32)
-
-    frame_mixed = frame_attention(
-        (project(0) * SCORE_SCALE).astype(jnp.bfloat16),
-        project(1).astype(jnp.bfloat16),
-        project(2).astype(jnp.bfloat16),
-    )
-    back = lax.all_to_all(
-        frame_mixed.reshape(head_size, rows_here, cols), "head", split_axis=0, concat_axis=0, tiled=True
-    ).reshape(view_here, shares, rows_here, cols)
-    added = jnp.dot(
-        jnp.transpose(back, (0, 2, 1, 3)).reshape(tokens_here, model_dim),
-        w_out_frame,
-        preferred_element_type=jnp.float32,
-    )
-    after_frame = (tokens.astype(jnp.float32).reshape(tokens_here, model_dim) + added).astype(
-        jnp.bfloat16
-    )
-
-    heads = model_dim // HEAD
-    copies = view_size * head_size // heads
-    normed = normalize(after_frame)
-    packed = lax.dot_general(
-        w_qkv_global, normed, (((0,), (1,)), ((), ())), preferred_element_type=jnp.float32
-    ).reshape(3, heads, HEAD, tokens_here)
-    scale = jnp.array([SCORE_SCALE, 1.0, 1.0], jnp.float32).reshape(3, 1, 1, 1)
-    packed = jnp.transpose((packed * scale).astype(jnp.bfloat16), (1, 0, 2, 3))
+    back = frame_attention(tokens, w_qkv_frame, head_size)
+    after_frame, packed = project_global(tokens, back, w_out_frame, w_qkv_global)
+
+    copies = view_size * head_size // (model_dim // HEAD)
     mixed = global_attention(
         packed, view_size // copies, copies, head_size, 1024
     ).reshape(model_dim, tokens_here)

time: 161 us -> 137 us (0.85)
  Pallas kernels: 100 us -> 134 us
  matrix products: 17.9 us -> 2.57 us
  waiting for transfers between devices: 13.7 us -> 0 us
  blocking collectives: 11.5 us -> 0 us
  other arithmetic: 7.86 us -> 0 us
  local copies, waits for them, and re-layouts: 5.31 us -> 0.01 us
  starting transfers between devices: 3.72 us -> 0 us
    pallas_call x1 -> x2, Pallas kernels: 7.56 us -> 40.3 us  [the longest x1 28 us: frame_attention(): pl.pallas_call(functools.partial(frame_kernel, shares), in_specs=[pl.Bloc...]
    dot_general x5 -> x0, matrix products: 15.4 us -> none  [the longest x3 8.21 us: project(): return jnp.dot(view_rows, weight, preferred_element_type=jnp.float32)]
    all_to_all x1 -> x0, waiting for transfers between devices: 13.7 us -> none  [on_device(): lax.all_to_all(sent, 'head', split_axis=0, concat_axis=0, tiled=True)]
    all_to_all x1 -> x0, blocking collectives: 11.5 us -> none  [on_device(): lax.all_to_all(frame_mixed.reshape(head_size, rows_here, cols), 'head', s...]
    all_to_all x1 -> x0, starting transfers between devices: 3.72 us -> none  [on_device(): lax.all_to_all(sent, 'head', split_axis=0, concat_axis=0, tiled=True)]
    transpose x1 -> x0, other arithmetic: 3.61 us -> none  [on_device(): packed = jnp.transpose((packed * scale).astype(jnp.bfloat16), (1, 0, 2, 3))]
    dot_general x1 -> x0, local copies, waits for them, and re-layouts: 3.56 us -> none  [on_device(): lax.dot_general(w_qkv_global, normed, (((0,), (1,)), ((), ())), preferred...]
    reduce_sum x3 -> x0, other arithmetic: 2.95 us -> none  [the longest x2 1.61 us: normalize(): spread = jnp.mean(jnp.square(widened - center), axis=-1, keepdims=True)]
  transfers between devices with their start and end apart: 1 -> 0, of which waited for: 1 -> 0; matrix products, arithmetic and copies ran while one was open for 0% -> 0% of each run, Pallas kernels for 0% -> 0%
where the time goes in v3:
time: 137 us
  Pallas kernels  134 us (98%)
  matrix products  2.57 us (2%)
    pallas_call x1, Pallas kernels, global_attention(): pl.pallas_call(functools.partial(global_kernel, planes, copies, per_plane...  93.8 us
    pallas_call x1, Pallas kernels, frame_attention(): pl.pallas_call(functools.partial(frame_kernel, shares), in_specs=[pl.Bloc...  28 us
    pallas_call x1, Pallas kernels, project_global(): pl.pallas_call(functools.partial(project_kernel, blocks), grid=(3 * block...  12.3 us

profile of v3, /device:TPU:16, one launch (start us, length us, event | category | flops | bytes accessed | tf_op | source)
XLA Modules:
  0.0 136.7 jit_solution(15390681020295557114)
XLA Ops:
  0.0 0.0 copy-start
  0.0 28.0 %frame_attention.1.back_ref = bf16[4,4,128,128]{3,2,1,0:T(8,128)(2,1)} custom-call(bf16[2,128,1024]{2,1,0:T(8,128)(2,1)} %tokens_ref.3, bf16[1024,3072]{1,0:T(8,128)(2,1)} %weight_ref.1), custom_call_target="tpu_custom_call" | custom-call | tf_op jit(solution)/shard_map/frame_attention/pallas_call | solution.py:145
  28.0 12.3 %project_global.1 = (bf16[256,1024]{1,0:T(8,128)(2,1)}, bf16[16,3,64,256]{3,2,1,0:T(8,128)(2,1)}) custom-call(bf16[2,128,1024]{2,1,0:T(8,128)(2,1)} %tokens_ref.3, bf16[4,4,128,128]{3,2,1,0:T(8,128)(2,1)} %frame_attention.1.back_ref, bf16[1024,1024]{1,0:T(8,128)(2,1)} %w_out_ref.1, bf16[1024,3072]{1,0:T(8,128)(2,1)} %w_qkv_ref.1), custom_call_target="tpu_custom_call" | custom-call | tf_op jit(solution)/shard_map/project_global/pallas_call | solution.py:211
  40.3 0.0 copy-start.1
  40.3 93.8 %global_attention.1 = bf16[16,64,256]{2,1,0:T(8,128)(2,1)} custom-call(bf16[16,3,64,256]{3,2,1,0:T(8,128)(2,1)} %get-tuple-element.8.packed), custom_call_target="tpu_custom_call" | custom-call | tf_op jit(solution)/shard_map/global_attention/pallas_call | solution.py:436
  134.1 0.0 copy-done
  134.1 0.0 copy-done.1
  134.1 2.6 %fusion = bf16[256,1024]{1,0:T(8,128)(2,1)} fusion(bf16[1024,256]{1,0:T(8,128)(2,1)} %bitcast.4, bf16[1024,1024]{1,0:T(8,128)(2,1)S(1)} %copy-done, bf16[256,1024]{1,0:T(8,128)(2,1)S(1)} %copy-done.1), kind=kOutput, calls=%fused_computation.1 | convolution fusion | flops 537657344 | bytes 3670016 | tf_op jit(solution)/shard_map/dot_general | solution.py:471
Async XLA Ops:
  0.0 134.1 %copy-start = (bf16[1024,1024]{1,0:T(8,128)(2,1)S(1)}, bf16[1024,1024]{1,0:T(8,128)(2,1)}, u32[]{:S(2)}) copy-start(bf16[1024,1024]{1,0:T(8,128)(2,1)} %param.9) | copy-start | bytes 6291460
  40.3 93.8 %copy-start.1 = (bf16[256,1024]{1,0:T(8,128)(2,1)S(1)}, bf16[256,1024]{1,0:T(8,128)(2,1)}, u32[]{:S(2)}) copy-start(bf16[256,1024]{1,0:T(8,128)(2,1)} %get-tuple-element.7) | copy-start | bytes 1572868

commit v4 on v3

--- a/solution.py
+++ b/solution.py
@@ -430,7 +430,7 @@
     heads, _, head, width = packed.shape
     stage_rows = per_plane * width
     rows = planes * stage_rows
-    key_step = min(key_step, stage_rows)
+    key_step = min(key_step, copies * stage_rows)
     dma = pltpu.SemaphoreType.DMA
     hops = max(1, copies - 1)
     return pl.pallas_call(
@@ -466,7 +466,7 @@
 
     copies = view_size * head_size // (model_dim // HEAD)
     mixed = global_attention(
-        packed, view_size // copies, copies, head_size, 1024
+        packed, view_size // copies, copies, head_size, 2048
     ).reshape(model_dim, tokens_here)
     added = lax.dot_general(
         mixed, w_out_global, (((0,), (0,)), ((), ())), preferred_element_type=jnp.float32

time: 137 us -> 135 us (0.985)
  Pallas kernels: 134 us -> 132 us
    pallas_call x1, Pallas kernels: 93.8 us -> 91.4 us  [global_attention(): pl.pallas_call(functools.partial(global_kernel, planes, copies, per_plane...]
where the time goes in v4:
time: 135 us; the launch traced here: 134 us
  Pallas kernels  132 us (98%)
  matrix products  2.56 us (2%)
    pallas_call x1, Pallas kernels, global_attention(): pl.pallas_call(functools.partial(global_kernel, planes, copies, per_plane...  91.4 us
    pallas_call x1, Pallas kernels, frame_attention(): pl.pallas_call(functools.partial(frame_kernel, shares), in_specs=[pl.Bloc...  28 us
    pallas_call x1, Pallas kernels, project_global(): pl.pallas_call(functools.partial(project_kernel, blocks), grid=(3 * block...  12.3 us

profile of v4, /device:TPU:16, one launch (start us, length us, event | category | flops | bytes accessed | tf_op | source)
XLA Modules:
  0.0 134.3 jit_solution(6439611495671085114)
XLA Ops:
  0.0 0.0 copy-start
  0.0 28.0 %frame_attention.1.back_ref = bf16[4,4,128,128]{3,2,1,0:T(8,128)(2,1)} custom-call(bf16[2,128,1024]{2,1,0:T(8,128)(2,1)} %tokens_ref.3, bf16[1024,3072]{1,0:T(8,128)(2,1)} %weight_ref.1), custom_call_target="tpu_custom_call" | custom-call | tf_op jit(solution)/shard_map/frame_attention/pallas_call | solution.py:145
  28.0 12.3 %project_global.1 = (bf16[256,1024]{1,0:T(8,128)(2,1)}, bf16[16,3,64,256]{3,2,1,0:T(8,128)(2,1)}) custom-call(bf16[2,128,1024]{2,1,0:T(8,128)(2,1)} %tokens_ref.3, bf16[4,4,128,128]{3,2,1,0:T(8,128)(2,1)} %frame_attention.1.back_ref, bf16[1024,1024]{1,0:T(8,128)(2,1)} %w_out_ref.1, bf16[1024,3072]{1,0:T(8,128)(2,1)} %w_qkv_ref.1), custom_call_target="tpu_custom_call" | custom-call | tf_op jit(solution)/shard_map/project_global/pallas_call | solution.py:211
  40.3 0.0 copy-start.1
  40.3 91.4 %global_attention.1 = bf16[16,64,256]{2,1,0:T(8,128)(2,1)} custom-call(bf16[16,3,64,256]{3,2,1,0:T(8,128)(2,1)} %get-tuple-element.8.packed), custom_call_target="tpu_custom_call" | custom-call | tf_op jit(solution)/shard_map/global_attention/pallas_call | solution.py:436
  131.7 0.0 copy-done
  131.8 0.0 copy-done.1
  131.8 2.6 %fusion = bf16[256,1024]{1,0:T(8,128)(2,1)} fusion(bf16[1024,256]{1,0:T(8,128)(2,1)} %bitcast.4, bf16[1024,1024]{1,0:T(8,128)(2,1)S(1)} %copy-done, bf16[256,1024]{1,0:T(8,128)(2,1)S(1)} %copy-done.1), kind=kOutput, calls=%fused_computation.1 | convolution fusion | flops 537657344 | bytes 3670016 | tf_op jit(solution)/shard_map/dot_general | solution.py:471
Async XLA Ops:
  0.0 131.7 %copy-start = (bf16[1024,1024]{1,0:T(8,128)(2,1)S(1)}, bf16[1024,1024]{1,0:T(8,128)(2,1)}, u32[]{:S(2)}) copy-start(bf16[1024,1024]{1,0:T(8,128)(2,1)} %param.9) | copy-start | bytes 6291460
  40.3 91.5 %copy-start.1 = (bf16[256,1024]{1,0:T(8,128)(2,1)S(1)}, bf16[256,1024]{1,0:T(8,128)(2,1)}, u32[]{:S(2)}) copy-start(bf16[256,1024]{1,0:T(8,128)(2,1)} %get-tuple-element.7) | copy-start | bytes 1572868
